TPU v7x, 32 devices: a whole 2x2x4 slice. The times are simulated.
32 devices in a mesh: dp: 8 (over z, core), ctx: 4 (over y, x).
Axes of the slice: x: 2, y: 2, z: 4, core: 2. Of those that a mesh axis runs over, the one named last changes fastest.
Arguments:
- loader_rows: bfloat16 [8192, 512], P(('dp', 'ctx')), may hold values from -60 to 60
- send_slot: int32 [8192], P(('dp', 'ctx')), may hold values from 0 to 383, as said below
- arrive_slot: int32 [8192], P(('dp', 'ctx')), may hold values from 0 to 383, as said below
- user_lengths: int32 [8, 4], P('dp'), may hold values from 1 to 768, 1024 in all within a row
- proj_weight: bfloat16 [512, 2048], replicated, may hold values from -0.25 to 0.25
- out_weight: bfloat16 [512, 512], replicated, may hold values from -0.25 to 0.25
- cotangent: bfloat16 [8192, 512], P(('dp', 'ctx')), may hold values from -6 to 6
Outputs:
- layer_out: bfloat16 [8192, 512], P(('dp', 'ctx'))
- row_grads: bfloat16 [8192, 512], P(('dp', 'ctx'))
- proj_grad: float32 [512, 2048], replicated
- out_grad: float32 [512, 512], replicated
Inputs may be any that keep to these rules, and one draw needn't show every extreme that they name: `send_slot`: on each loader device its 256 entries are distinct slots d * 12 + k, d the owner device and k counting that owner's rows from this loader from 0; no loader sends more than 12 rows to one owner and some pairs send exactly 12; the number of rows from loader s to owner d depends only on (d - s) mod (8 * 4). `arrive_slot`: on each owner device its 256 entries are distinct slots s * 12 + k, the k-th row that loader s sends to it; every owner receives exactly 256 rows.
All inputs are finite; a program needn't handle non-finite values.
Results may differ from a plain program's by a relative error of at most 0.009.
Values may be sent and summed in bfloat16 or wider, within the bound.
No kernel may reach another device: no remote copies, remote signals or barrier semaphores. Data moves between devices by JAX's collectives and lax.ppermute only.
A program may use at most 128 MiB of HBM per device.

v0:
```python
import functools

import jax
import jax.numpy as jnp
from jax import lax
from jax.experimental import pallas as pl
from jax.experimental.pallas import tpu as pltpu
from jax.sharding import PartitionSpec as P


HEADS = 8
EPS = 1e-05
TILE = 256
BF = jnp.bfloat16
F32 = jnp.float32
SRC_SHIFT = 16
LOW = 128
EXTRA = 16


def bits_of(count):
    return [1 << each for each in range(count.bit_length() - 1)]


def reverse_bits(value, count):
    width = count.bit_length() - 1
    result = 0
    for each in range(width):
        result = result | (((value >> each) & 1) << (width - 1 - each))
    return result


def swap(values, axis, distance):
    size = lax.axis_size(axis)
    return lax.ppermute(values, axis, [(each, each ^ distance) for each in range(size)])


def spread(values, axis, order):
    held = {0: values}
    for bit in order:
        held.update({key | bit: swap(held[key], axis, bit) for key in sorted(held)})
    return held


def direct(parts, axis):
    return [parts[0]] + [swap(parts[rel], axis, rel) for rel in range(1, len(parts))]


def nt_dot(left, right):
    return lax.dot_general(left, right, (((1,), (1,)), ((), ())), preferred_element_type=F32)


def tn_dot(left, right):
    return lax.dot_general(left, right, (((0,), (0,)), ((), ())), preferred_element_type=F32)


def nn_dot(left, right):
    return jnp.dot(left, right, preferred_element_type=F32)


def normalize(values):
    centre = values - jnp.mean(values, axis=-1, keepdims=True)
    inverse = lax.rsqrt(jnp.mean(centre * centre, axis=-1, keepdims=True) + EPS)
    return centre * inverse, inverse


def silu(values):
    half = 0.5 * values
    return half + half * jnp.tanh(half)


def silu_grad(values):
    half = 0.5 * values
    tanh = jnp.tanh(half)
    return (0.5 + 0.5 * tanh) * (1.0 + half * (1.0 - tanh))


def call(kernel, out_shapes, args, flops, smem=(), hbm=(), limit=16):
    moved = sum(each.size * each.dtype.itemsize for each in list(args) + list(out_shapes))
    specs = [
        pl.BlockSpec(
            memory_space=pltpu.SMEM if index in smem else pltpu.HBM if index in hbm else pltpu.VMEM
        )
        for index in range(len(args))
    ]
    return functools.partial(
        pl.pallas_call,
        kernel,
        out_shape=tuple(out_shapes),
        in_specs=specs,
        out_specs=tuple(pl.BlockSpec(memory_space=pltpu.VMEM) for _ in out_shapes),
        compiler_params=pltpu.CompilerParams(vmem_limit_bytes=limit * 1024 * 1024),
        cost_estimate=pl.CostEstimate(flops=flops, bytes_accessed=moved, transcendentals=0),
    )


def local(loader_rows, send_slot, arrive_slot, user_lengths, proj_weight, out_weight, cotangent):
    own_count = send_slot.shape[0]
    width = out_weight.shape[0]
    users = user_lengths.shape[1]
    ctx = lax.axis_size("ctx")
    dps = lax.axis_size("dp")
    devices = ctx * dps
    per_pair = own_count // devices
    cap = per_pair + max(1, per_pair // 2)
    half = own_count // 2
    rows_all = ctx * own_count
    blocks = 2 * ctx
    part = width // ctx
    heads = HEADS // ctx
    head_dim = width // HEADS
    scale = head_dim ** (-0.5)
    pair_rows = ctx * cap
    side_rows = dps // 2 * pair_rows
    tiles = rows_all // TILE
    ctx_bits = bits_of(ctx)
    me_ctx = lax.axis_index("ctx")
    me_dp = lax.axis_index("dp")
    shape = jax.ShapeDtypeStruct
    dp_bits = bits_of(dps)
    proj_step, out_step = width // dps, part // dps
    piece_rows = 2 * proj_step + ctx // 2 * out_step
    packed = part % 128 == 0 and out_step % 16 == 0
    room = max(20, 20 * rows_all // 1024)
    grad_scale = (own_count * devices) ** (-0.5)

    def block_of(device, side):
        return device if side == 0 else blocks - 1 - device

    def block_rows(device, side):
        return pl.ds(pl.multiple_of(block_of(device, side) * half, half), half)

    def weight_of(ref, column, each):
        if packed:
            return ref[:, pl.ds(pl.multiple_of(each * width + column * part, part), part)]
        return ref[column, :, each * part : (each + 1) * part]

    weights = proj_weight
    if not packed:
        weights = (
            proj_weight.reshape(width, 4, ctx, part).transpose(2, 0, 1, 3).reshape(ctx, width, 4 * part)
        )

    def pack_kernel(slot_hbm, rows_hbm, arrive_hbm, cot_hbm, *refs):
        out_refs, (slot_ref, rows_ref, arrive_ref, sems) = refs[: dps + 1], refs[dps + 1 :]
        mine = lax.axis_index("dp")
        copies = [
            pltpu.make_async_copy(start, end, sems.at[at])
            for at, (start, end) in enumerate(
                (
                    (slot_hbm, slot_ref),
                    (rows_hbm, rows_ref),
                    (arrive_hbm, arrive_ref),
                    (cot_hbm, out_refs[dps].at[pl.ds(0, own_count), :]),
                )
            )
        ]
        for each in copies:
            each.start()
        for each in copies:
            each.wait()
        slot = slot_ref[...]
        rows = rows_ref[...]
        row_id = lax.broadcasted_iota(jnp.int32, (pair_rows, own_count), 0)
        for rel in range(dps):
            picked = (row_id + (mine ^ rel) * pair_rows == slot).astype(BF)
            out_refs[rel][...] = nn_dot(picked, rows).astype(BF)
        cot_ref = out_refs[dps]
        arrive = arrive_ref[...]
        source = jnp.floor((arrive.astype(F32) + 0.5) * (1.0 / cap)).astype(jnp.int32)
        place = arrive - source * cap
        base = ((source >> len(ctx_bits)) ^ mine) * pair_rows + lax.axis_index("ctx") * cap + place
        line = lax.broadcasted_iota(jnp.int32, (EXTRA, own_count), 0)
        table = jnp.where(
            line == 0, source & (ctx - 1), jnp.where(line == 1, base // LOW, base % LOW)
        )
        cot_ref[own_count:, :] = jnp.zeros((EXTRA, width), BF)
        cot_ref[own_count:, :own_count] = table.astype(F32).astype(BF)

    pack_args = (
        send_slot.reshape(1, own_count),
        loader_rows,
        arrive_slot.reshape(1, own_count),
        cotangent,
    )
    pack_outs = [shape((pair_rows, width), BF)] * dps + [shape((own_count + EXTRA, width), BF)]
    *sent, cot_own = call(
        pack_kernel, pack_outs, pack_args, 2 * dps * pair_rows * own_count * width, hbm=range(4), limit=60
    )(
        scratch_shapes=[
            pltpu.VMEM((1, own_count), jnp.int32),
            pltpu.VMEM((own_count, width), BF),
            pltpu.VMEM((1, own_count), jnp.int32),
            pltpu.SemaphoreType.DMA((4,)),
        ]
    )(*pack_args)
    cot_of = direct([cot_own] * ctx, "ctx")
    landed = direct(sent, "dp")
    sides = (
        spread(jnp.concatenate(landed[: dps // 2]), "ctx", ctx_bits),
        spread(jnp.concatenate(landed[dps // 2 :]), "ctx", ctx_bits[::-1]),
    )

    def prepare_kernel(lengths_ref, weight_ref, out_weight_ref, own_ref, out_own_ref, begin_ref):
        mine = lax.axis_index("ctx")
        for each in range(4):
            own_ref[:, each * part : (each + 1) * part] = weight_of(weight_ref, mine, each)
        out_own_ref[...] = out_weight_ref[pl.ds(pl.multiple_of(mine * part, part), part), :]
        position = lax.broadcasted_iota(jnp.int32, (blocks, half), 0) * half + lax.broadcasted_iota(
            jnp.int32, (blocks, half), 1
        )
        end = 0
        begin = jnp.zeros((blocks, half), jnp.int32)
        for each in range(users):
            length = lengths_ref[0, each]
            end = end + length
            begin = begin + jnp.where(position >= end, length, 0)
        begin_ref[...] = begin

    prepare_args = (user_lengths, weights, out_weight)
    prepare_outs = [shape((width, 4 * part), BF), shape((part, width), BF), shape((blocks, half), jnp.int32)]
    proj_own, out_own, begin_of = call(prepare_kernel, prepare_outs, prepare_args, width * width, smem=(0,))()(
        *prepare_args
    )

    def lane_masks():
        lane = lax.broadcasted_iota(jnp.int32, (1, part), 1)
        return [
            (lane >= each * head_dim) & (lane < (each + 1) * head_dim) for each in range(heads)
        ]

    def forward_kernel(*refs):
        side_refs = (refs[:ctx], refs[ctx : 2 * ctx])
        cot_refs = refs[2 * ctx : 3 * ctx]
        begin_ref, own_weight_ref, out_own_ref = refs[3 * ctx : 3 * ctx + 3]
        own_ref, norm_t_ref, pre_ref, proj_ref, att_ref, gg_ref, stat_ref = refs[3 * ctx + 3 : 3 * ctx + 10]
        where_ref, rows_ref, query_ref, value_ref = refs[3 * ctx + 10 :]
        mine = lax.axis_index("ctx")
        out_own = out_own_ref[...]
        begins = jnp.transpose(begin_ref[...].astype(F32)).astype(jnp.int32)
        for rel in range(ctx):
            table = jnp.transpose(cot_refs[rel][own_count:, :own_count].astype(F32)[:8, :])
            column = (table[:, 0:1].astype(jnp.int32) << SRC_SHIFT) + (
                table[:, 1:2] * LOW + table[:, 2:3]
            ).astype(jnp.int32)
            for side in range(2):
                here = slice(side * half, (side + 1) * half)
                where_ref[block_rows(mine ^ rel, side), :] = column[here, :]
                gg_ref[block_rows(mine ^ rel, side), :] = nt_dot(cot_refs[rel][here, :], out_own)
        masks = lane_masks()
        source_row = lax.broadcasted_iota(jnp.int32, (TILE, side_rows), 1)
        for tile in range(tiles):
            span = pl.ds(tile * TILE, TILE)
            wanted = where_ref[span, :]
            total = jnp.zeros((TILE, width), F32)
            for rel in range(ctx):
                for side in range(2):
                    key = source_row + (((mine ^ rel) << SRC_SHIFT) + side * side_rows)
                    picked = (key == wanted).astype(BF)
                    total = total + nn_dot(picked, side_refs[side][rel][...])
            rows_ref[span, :] = total.astype(BF)
            normed = normalize(total)[0].astype(BF)
            norm_t_ref[:, tile * TILE : (tile + 1) * TILE] = jnp.transpose(normed)
            pre = nn_dot(normed, own_weight_ref[...])
            pre_ref[span, :] = pre
            proj = silu(pre).astype(BF)
            proj_ref[span, :] = proj
            query = proj[:, 2 * part : 3 * part] * jnp.asarray(0.5 * scale, BF)
            value = proj[:, part : 2 * part]
            for head in range(heads):
                query_ref[head, span, :] = jnp.where(masks[head], query, jnp.zeros_like(query))
                value_ref[head, span, :] = jnp.where(masks[head], value, jnp.zeros_like(value))
        for side in range(2):
            own_ref[side * half : (side + 1) * half, :] = rows_ref[block_rows(mine, side), :]
        for at in range(tiles):
            span = pl.ds(at * TILE, TILE)
            query_pos = lax.broadcasted_iota(jnp.int32, (TILE, 1), 0) + at * TILE
            begin = jnp.concatenate(
                [begins[:, each : each + 1] for each in range(at * TILE // half, (at + 1) * TILE // half)]
            )
            total = jnp.zeros((TILE, part), F32)
            for key_at in range(at + 1):
                key_span = pl.ds(key_at * TILE, TILE)
                key_pos = lax.broadcasted_iota(jnp.int32, (1, TILE), 1) + key_at * TILE
                allowed = key_pos >= begin
                if key_at == at:
                    allowed = allowed & (key_pos <= query_pos)
                key = proj_ref[key_span, 3 * part :]
                for head in range(heads):
                    score = nt_dot(query_ref[head, span, :], key)
                    weight = jnp.where(allowed, score + score * jnp.tanh(score), 0.0).astype(BF)
                    total = total + nn_dot(weight, value_ref[head, key_span, :])
            att_ref[span, :] = total
            grad = gg_ref[span, :] * proj_ref[span, :part].astype(F32)
            mean = jnp.mean(total, axis=-1, keepdims=True)
            centre = total - mean
            spread_sum = jnp.sum(centre * centre, axis=-1, keepdims=True)
            grad_sum = jnp.sum(grad, axis=-1, keepdims=True)
            cross_sum = jnp.sum(grad * centre, axis=-1, keepdims=True)
            lane = lax.broadcasted_iota(jnp.int32, (TILE, 128), 1)
            table = jnp.where(
                lane == 0, mean, jnp.where(lane == 1, spread_sum, jnp.where(lane == 2, grad_sum, cross_sum))
            )
            for sub in range(TILE // half):
                turned = jnp.transpose(table[sub * half : (sub + 1) * half, :])
                block = at * (TILE // half) + sub
                for each in range(4):
                    stat_ref[each, block : block + 1, :] = turned[each : each + 1, :]

    fwd_args = (
        tuple(sides[0][rel] for rel in range(ctx))
        + tuple(sides[1][rel] for rel in range(ctx))
        + tuple(cot_of)
        + (begin_of, proj_own, out_own)
    )
    fwd_outs = [
        shape((own_count, width), BF),
        shape((width, rows_all), BF),
        shape((rows_all, 4 * part), F32),
        shape((rows_all, 4 * part), BF),
        shape((rows_all, part), F32),
        shape((rows_all, part), F32),
        shape((4, blocks, half), F32),
    ]
    own_rows, norm_t, pre, proj, attended, grad_gated, stats = call(
        forward_kernel, fwd_outs, fwd_args, 4 * rows_all * rows_all * part, limit=room
    )(
        scratch_shapes=[
            pltpu.VMEM((rows_all, 1), jnp.int32),
            pltpu.VMEM((rows_all, width), BF),
            pltpu.VMEM((heads, rows_all, part), BF),
            pltpu.VMEM((heads, rows_all, part), BF),
        ]
    )(*fwd_args)

    stats_of = direct([stats] * ctx, "ctx")

    grad_count = 4 if packed else 2

    def proj_places(chunk):
        return [(at * proj_step, 2 * chunk + at) for at in range(2)]

    def out_places(chunk):
        return [(2 * proj_step + at * out_step, ctx // 2 * chunk + at) for at in range(ctx // 2)]

    def backward_kernel(*refs):
        stat_refs, cot_refs = refs[:ctx], refs[ctx : 2 * ctx]
        begin_ref, att_ref, gg_ref, pre_ref, proj_ref, norm_t_ref = refs[2 * ctx : 2 * ctx + 6]
        grad_refs, refs = refs[2 * ctx + 6 : 2 * ctx + 6 + grad_count], refs[2 * ctx + 6 + grad_count :]
        row_refs = refs[:ctx]
        query_ref, key_ref, grad_ref, dq_ref, gp_ref, gated_ref, late_ref, out_ref = refs[ctx:]
        mine = lax.axis_index("ctx")
        masks = lane_masks()

        def masked(values, head):
            return jnp.where(masks[head], values, jnp.zeros_like(values))

        means = [each[0] for each in stat_refs]
        mean = sum(means) / ctx
        spread_sum = sum(each[1] + part * (own - mean) ** 2 for each, own in zip(stat_refs, means))
        inverse = lax.rsqrt(spread_sum / width + EPS)
        grad_mean = sum(each[2] for each in stat_refs) / width
        cross = sum(each[3] + each[2] * (own - mean) for each, own in zip(stat_refs, means))
        cross_mean = inverse * cross / width
        for block in range(blocks):
            span = pl.ds(block * half, half)
            table = jnp.concatenate(
                [each[block : block + 1, :] for each in (mean, inverse, grad_mean, cross_mean)] * 2
            )
            columns = jnp.transpose(table)
            mean_c, inverse_c, grad_c, cross_c = (columns[:, each : each + 1] for each in range(4))
            normed = (att_ref[span, :] - mean_c) * inverse_c
            grad = gg_ref[span, :]
            update = proj_ref[span, :part].astype(F32)
            gated_ref[span, :] = (normed * update).astype(BF)
            grad_att = ((grad * update - grad_c - normed * cross_c) * inverse_c).astype(BF)
            gp_ref[span, :part] = (grad * normed * silu_grad(pre_ref[span, :part])).astype(BF)
            query = proj_ref[span, 2 * part : 3 * part] * jnp.asarray(0.5 * scale, BF)
            for head in range(heads):
                query_ref[head, span, :] = masked(query, head)
                key_ref[head, span, :] = masked(proj_ref[span, 3 * part :], head)
                grad_ref[head, span, :] = masked(grad_att, head)
            dq_ref[span, :] = jnp.zeros((half, part), F32)
        out_term = jnp.zeros((part, width), F32)
        for rel in range(ctx):
            for side in range(2):
                here = slice(side * half, (side + 1) * half)
                gated = gated_ref[block_rows(mine ^ rel, side), :]
                row_refs[rel][here, 4 * part :] = gated
            out_term = out_term + tn_dot(row_refs[rel][:, 4 * part :], cot_refs[rel][:own_count, :])
        out_ref[...] = out_term.astype(BF)
        for key_at in range(tiles):
            key_span = pl.ds(key_at * TILE, TILE)
            key_pos = lax.broadcasted_iota(jnp.int32, (TILE, 1), 0) + key_at * TILE
            key = proj_ref[key_span, 3 * part :]
            value = proj_ref[key_span, part : 2 * part] * jnp.asarray(0.5 * scale, BF)
            grad_key = jnp.zeros((TILE, part), F32)
            grad_value = jnp.zeros((TILE, part), F32)
            for at in range(key_at, tiles):
                span = pl.ds(at * TILE, TILE)
                query_pos = lax.broadcasted_iota(jnp.int32, (1, TILE), 1) + at * TILE
                begin = jnp.concatenate(
                    [
                        begin_ref[each : each + 1, :]
                        for each in range(at * TILE // half, (at + 1) * TILE // half)
                    ],
                    axis=1,
                )
                allowed = key_pos >= begin
                if at == key_at:
                    allowed = allowed & (key_pos <= query_pos)
                grad_query = jnp.zeros((TILE, part), F32)
                for head in range(heads):
                    score = nt_dot(key, query_ref[head, span, :])
                    tanh = jnp.tanh(score)
                    cross = score * tanh
                    weight = jnp.where(allowed, score + cross, 0.0).astype(BF)
                    grad_value = grad_value + nn_dot(weight, grad_ref[head, span, :])
                    grad_weight = nt_dot(value, grad_ref[head, span, :])
                    slope = (1.0 + tanh) * (1.0 + score - cross)
                    grad_score = jnp.where(allowed, grad_weight * slope, 0.0).astype(BF)
                    grad_key = grad_key + nn_dot(grad_score, query_ref[head, span, :])
                    grad_query = grad_query + tn_dot(grad_score, key_ref[head, key_span, :])
                dq_ref[span, :] = dq_ref[span, :] + grad_query
            gp_ref[key_span, part : 2 * part] = (
                grad_value * silu_grad(pre_ref[key_span, part : 2 * part])
            ).astype(BF)
            gp_ref[key_span, 3 * part :] = (
                grad_key * (2.0 / scale) * silu_grad(pre_ref[key_span, 3 * part :])
            ).astype(BF)
        for tile in range(tiles):
            span = pl.ds(tile * TILE, TILE)
            gp_ref[span, 2 * part : 3 * part] = (
                dq_ref[span, :] * silu_grad(pre_ref[span, 2 * part : 3 * part])
            ).astype(BF)
        for rel in range(ctx):
            for side in range(2):
                row_refs[rel][side * half : (side + 1) * half, : 4 * part] = gp_ref[
                    block_rows(mine ^ rel, side), :
                ]
        late_ref[...] = nn_dot(norm_t_ref[...], gp_ref[...]).astype(BF)
        if not packed:
            grad_refs[0][...] = late_ref[...]
            grad_refs[1][...] = out_ref[...]
            return
        mine = lax.axis_index("dp")
        for slot in range(dps):
            index = reverse_bits(slot, dps) ^ mine
            rows = pl.ds(pl.multiple_of(index * proj_step, proj_step), proj_step)
            out_rows = pl.ds(pl.multiple_of(index * out_step, out_step), out_step)
            for chunk in range(2):
                to = grad_refs[2 * chunk + slot // (dps // 2)].at[slot % (dps // 2)]
                for first, each in proj_places(chunk):
                    to[first : first + proj_step, :] = late_ref[rows, each * part : (each + 1) * part]
                for first, each in out_places(chunk):
                    to[first : first + out_step, :] = out_ref[out_rows, each * part : (each + 1) * part]

    bwd_args = (*stats_of, *cot_of, begin_of, attended, grad_gated, pre, proj, norm_t)
    if packed:
        bwd_outs = [shape((dps // 2, piece_rows, part), BF)] * 4
    else:
        bwd_outs = [shape((width, 4 * part), BF), shape((part, width), BF)]
    bwd_outs = bwd_outs + [shape((own_count, 5 * part), BF)] * ctx
    results = call(
        backward_kernel, bwd_outs, bwd_args, 10 * rows_all * rows_all * part, limit=room
    )(
        scratch_shapes=[
            pltpu.VMEM((heads, rows_all, part), BF),
            pltpu.VMEM((heads, rows_all, part), BF),
            pltpu.VMEM((heads, rows_all, part), BF),
            pltpu.VMEM((rows_all, part), F32),
            pltpu.VMEM((rows_all, 4 * part), BF),
            pltpu.VMEM((rows_all, part), BF),
            pltpu.VMEM((width, 4 * part), BF),
            pltpu.VMEM((part, width), BF),
        ]
    )(*bwd_args)

    grad_parts, row_parts = results[:grad_count], results[grad_count:]

    if not packed:
        rev = jnp.array([reverse_bits(each, dps) for each in range(dps)], jnp.int32)
        proj_blocks = grad_parts[0].reshape(dps, proj_step, 4, part).transpose(0, 2, 1, 3)
        out_blocks = grad_parts[1].reshape(dps, out_step, ctx, part).transpose(0, 2, 1, 3)
        grad_parts = []
        for chunk in range(2):
            pieces = jnp.concatenate(
                [
                    proj_blocks[:, 2 * chunk : 2 * chunk + 2].reshape(dps, -1, part),
                    out_blocks[:, ctx // 2 * chunk : ctx // 2 * (chunk + 1)].reshape(dps, -1, part),
                ],
                axis=1,
            )
            grad_parts += jnp.split(jnp.take(pieces, rev ^ me_dp, axis=0), 2)

    def add_kernel(keep_ref, got_ref, *out_refs):
        count = out_refs[0].shape[0]
        for at, ref in enumerate(out_refs):
            here = slice(at * count, (at + 1) * count)
            ref[...] = (keep_ref[here].astype(F32) + got_ref[here].astype(F32)).astype(BF)

    def exchange_kernel(keep_ref, got_ref, out_ref):
        for at in range(2):
            total = keep_ref[at].astype(F32) + got_ref[1 - at].astype(F32)
            out_ref[at] = total.astype(BF)

    def reduce_dp(keep, send):
        for bit in dp_bits[:-1]:
            got = swap(send, "dp", bit)
            count = keep.shape[0] // 2
            last = count == 1
            outs = [shape((2 if last else count, piece_rows, part), BF)] * (1 if last else 2)
            keep, *send = call(add_kernel, outs, (keep, got), keep.size)()(keep, got)
            send = send[0] if send else None
        got = swap(keep, "dp", dp_bits[-1])
        return call(exchange_kernel, [shape(keep.shape, BF)], (keep, got), keep.size)()(keep, got)[0]

    held = [reduce_dp(*grad_parts[2 * chunk : 2 * chunk + 2]) for chunk in range(2)]
    keys = [0, dp_bits[-1]]
    row_own = direct(row_parts, "ctx")

    def rows_kernel(*refs):
        part_refs, (rows_ref, cot_ref, weight_ref, out_weight_ref, layer_ref, grad_ref) = refs[:ctx], refs[ctx:]
        mine = lax.axis_index("ctx")
        rows = rows_ref[...].astype(F32)
        layer = rows
        grad = jnp.zeros((own_count, width), F32)
        for rel in range(ctx):
            column = mine ^ rel
            at = pl.ds(pl.multiple_of(column * part, part), part)
            layer = layer + nn_dot(part_refs[rel][:, 4 * part :], out_weight_ref[at, :])
            for each in range(4):
                grad = grad + nt_dot(
                    part_refs[rel][:, each * part : (each + 1) * part], weight_of(weight_ref, column, each)
                )
        layer_ref[...] = layer.astype(BF)
        normed, inverse = normalize(rows)
        mean_grad = jnp.mean(grad, axis=-1, keepdims=True)
        mean_cross = jnp.mean(grad * normed, axis=-1, keepdims=True)
        back = (grad - mean_grad - normed * mean_cross) * inverse
        grad_ref[...] = (cot_ref[...].astype(F32) + back).astype(BF)

    rows_args = tuple(row_own) + (own_rows, cotangent, weights, out_weight)
    layer_out, row_grads = call(
        rows_kernel, [shape((own_count, width), BF)] * 2, rows_args, 10 * own_count * width * width
    )()(*rows_args)

    for bit in dp_bits[-2:0:-1]:
        held = [jnp.concatenate([each, swap(each, "dp", bit)]) for each in held]
        keys = keys + [key | bit for key in keys]
    order = (ctx_bits, ctx_bits[::-1])
    arrays, holds = [], []
    groups = [[], [], []]
    for chunk in range(2):
        for rel, values in spread(held[chunk], "ctx", order[chunk]).items():
            arrays.append(values)
            holds.append([(chunk, rel, key) for key in keys])
            groups[0 if rel == 0 else 2 if rel == ctx - 1 else 1].append(len(holds) - 1)
    for group in groups:
        both = jnp.concatenate([arrays[each] for each in group])
        arrays.append(swap(both, "dp", 1))
        holds.append([(chunk, rel, key | 1) for each in group for chunk, rel, key in holds[each]])

    if packed:

        def finish_kernel(*refs):
            proj_ref, out_ref = refs[len(arrays) :]
            mine_ctx, mine_dp = lax.axis_index("ctx"), lax.axis_index("dp")
            for ref, pieces in zip(refs, holds):
                for at, (chunk, rel_ctx, rel_dp) in enumerate(pieces):
                    column, index = mine_ctx ^ rel_ctx, mine_dp ^ rel_dp
                    rows = pl.ds(pl.multiple_of(index * proj_step, proj_step), proj_step)
                    for first, each in proj_places(chunk):
                        lanes = pl.ds(pl.multiple_of(each * width + column * part, part), part)
                        proj_ref[rows, lanes] = ref[at, first : first + proj_step, :].astype(F32) * grad_scale
                    rows = pl.ds(pl.multiple_of(column * part + index * out_step, out_step), out_step)
                    for first, each in out_places(chunk):
                        out_ref[rows, each * part : (each + 1) * part] = (
                            ref[at, first : first + out_step, :].astype(F32) * grad_scale
                        )

        proj_grad, out_grad = call(
            finish_kernel,
            [shape((width, 4 * width), F32), shape((width, width), F32)],
            arrays,
            width * width * 10,
        )()(*arrays)
        return (layer_out, row_grads, proj_grad, out_grad)

    pieces = {key: array[at] for array, hold in zip(arrays, holds) for at, key in enumerate(hold)}
    table = jnp.stack(
        [
            jnp.stack([jnp.stack([pieces[chunk, c, d] for chunk in range(2)]) for d in range(dps)])
            for c in range(ctx)
        ]
    )
    table = jnp.take(table, jnp.arange(ctx) ^ me_ctx, axis=0)
    table = jnp.take(table, jnp.arange(dps) ^ me_dp, axis=1).astype(F32) * grad_scale
    proj_grad = (
        table[:, :, :, : 2 * proj_step]
        .reshape(ctx, dps, 4, proj_step, part)
        .transpose(1, 3, 2, 0, 4)
        .reshape(width, 4 * width)
    )
    out_grad = (
        table[:, :, :, 2 * proj_step :]
        .reshape(ctx, dps, ctx, out_step, part)
        .transpose(0, 1, 3, 2, 4)
        .reshape(width, width)
    )
    return (layer_out, row_grads, proj_grad, out_grad)


def solution(mesh):
    placed = (
        P(("dp", "ctx"), None),
        P(("dp", "ctx")),
        P(("dp", "ctx")),
        P("dp", None),
        P(),
        P(),
        P(("dp", "ctx"), None),
    )

    return jax.shard_map(
        local,
        mesh=mesh,
        in_specs=placed,
        out_specs=(P(("dp", "ctx"), None), P(("dp", "ctx"), None), P(), P()),
        check_vma=False,
    )
```

profile of v0, /device:TPU:0, one launch (start us, length us, event | category | flops | bytes accessed | tf_op | source)
XLA Modules:
  0.0 121.4 jit_solution(11563603754883592681)
XLA Ops:
  0.6 2.3 %shard_map.102 = (bf16[48,512]{1,0:T(8,128)(2,1)}, bf16[48,512]{1,0:T(8,128)(2,1)}, bf16[48,512]{1,0:T(8,128)(2,1)}, bf16[48,512]{1,0:T(8,128)(2,1)}, bf16[48,51...) custom-call(s32[1,256]{1,0:T(1,128)} %bitcast.2, ...), custom_call_target="tpu_custom_call" | custom-call | flops 100663296 | bytes 1198080 | tf_op jit(solution)/shard_map/pallas_call | solution.py:187
  3.5 2.6 %collective-permute-start.1 = (bf16[48,512]{1,0:T(8,128)(2,1)}, bf16[48,512]{1,0:T(8,128)(2,1)S(1)}, u32[]{:S(2)}, u32[]{:S(2)}) collective-permute-start(bf16[48,512]{1,0:T(8,128)(2,1)} %get-tuple-element.41), channel_id=1, source_target_pairs={{0,8},{4,12},{8,0},{12,4},{16,24},{20,28},{24,16},{28,20},{1,9},{5... | collective-permute-start | bytes 147464 | tf_op jit(solution)/shard_map/ppermute | solution.py:35
  6.2 2.8 %collective-permute-start.6 = (bf16[48,512]{1,0:T(8,128)(2,1)}, bf16[48,512]{1,0:T(8,128)(2,1)S(1)}, u32[]{:S(2)}, u32[]{:S(2)}) collective-permute-start(bf16[48,512]{1,0:T(8,128)(2,1)} %get-tuple-element.43), channel_id=1, source_target_pairs={{0,16},{4,20},{8,24},{12,28},{16,0},{20,4},{24,8},{28,12},{1,17},{... | collective-permute-start | bytes 147464 | tf_op jit(solution)/shard_map/ppermute | solution.py:35
  8.9 0.8 constant_dynamic-update-slice_fusion.3
  9.8 3.6 %collective-permute-start.8 = (bf16[48,512]{1,0:T(8,128)(2,1)}, bf16[48,512]{1,0:T(8,128)(2,1)S(1)}, u32[]{:S(2)}, u32[]{:S(2)}) collective-permute-start(bf16[48,512]{1,0:T(8,128)(2,1)} %get-tuple-element.45), channel_id=1, source_target_pairs={{0,24},{4,28},{8,16},{12,20},{16,8},{20,12},{24,0},{28,4},{1,25},{... | collective-permute-start | bytes 147464 | tf_op jit(solution)/shard_map/ppermute | solution.py:35
  13.5 1.6 %collective-permute-start.4 = (bf16[192,512]{1,0:T(8,128)(2,1)S(1)}, bf16[192,512]{1,0:T(8,128)(2,1)S(1)}, u32[]{:S(2)}, u32[]{:S(2)}) collective-permute-start(bf16[192,512]{1,0:T(8,128)(2,1)S(1)} %constant_dynamic-update-slice_fusion.refs_0_), channel_id=1, source_target_pairs={{0,2},{1,3},{2,0},{3,1},{4,6},{5,7},{6,4},{7,5},{8,10},{9,11},{10,... | collective-permute-start | bytes 589832 | tf_op jit(solution)/shard_map/ppermute | solution.py:35
  15.1 1.5 %collective-permute-start.3 = (bf16[192,512]{1,0:T(8,128)(2,1)S(1)}, bf16[192,512]{1,0:T(8,128)(2,1)S(1)}, u32[]{:S(2)}, u32[]{:S(2)}) collective-permute-start(bf16[192,512]{1,0:T(8,128)(2,1)S(1)} %constant_dynamic-update-slice_fusion.refs_0_), channel_id=1, source_target_pairs={{0,1},{1,0},{2,3},{3,2},{4,5},{5,4},{6,7},{7,6},{8,9},{9,8},{10,11... | collective-permute-start | bytes 589832 | tf_op jit(solution)/shard_map/ppermute | solution.py:35
  16.6 2.6 %collective-permute-done.9 = bf16[48,512]{1,0:T(8,128)(2,1)S(1)} collective-permute-done((bf16[48,512]{1,0:T(8,128)(2,1)}, bf16[48,512]{1,0:T(8,128)(2,1)S(1)}, u32[]{:S(2)}, u32[]{:S(2)}) %collective-permute-start.9) | collective-permute-done | bytes 49184 | tf_op jit(solution)/shard_map/ppermute | solution.py:35
  19.3 1.5 %collective-permute-start.11 = (bf16[192,512]{1,0:T(8,128)(2,1)S(1)}, bf16[192,512]{1,0:T(8,128)(2,1)S(1)}, u32[]{:S(2)}, u32[]{:S(2)}) collective-permute-start(bf16[192,512]{1,0:T(8,128)(2,1)S(1)} %constant_dynamic-update-slice_fusion.4.refs_4_), channel_id=1, source_target_pairs={{0,2},{1,3},{2,0},{3,1},{4,6},{5,7},{6,4},{7,5},{8,10},{9,11},{10,... | collective-permute-start | bytes 589832 | tf_op jit(solution)/shard_map/ppermute | solution.py:35
  20.8 1.5 %collective-permute-start.10 = (bf16[192,512]{1,0:T(8,128)(2,1)S(1)}, bf16[192,512]{1,0:T(8,128)(2,1)S(1)}, u32[]{:S(2)}, u32[]{:S(2)}) collective-permute-start(bf16[192,512]{1,0:T(8,128)(2,1)S(1)} %constant_dynamic-update-slice_fusion.4.refs_4_), channel_id=1, source_target_pairs={{0,1},{1,0},{2,3},{3,2},{4,5},{5,4},{6,7},{7,6},{8,9},{9,8},{10,11... | collective-permute-start | bytes 589832 | tf_op jit(solution)/shard_map/ppermute | solution.py:35
  22.8 1.5 %collective-permute-start.14 = (bf16[272,512]{1,0:T(8,128)(2,1)}, bf16[272,512]{1,0:T(8,128)(2,1)S(1)}, u32[]{:S(2)}, u32[]{:S(2)}) collective-permute-start(bf16[272,512]{1,0:T(8,128)(2,1)} %get-tuple-element.47.refs_8_.refs_4_), channel_id=1, source_target_pairs={{0,2},{1,3},{2,0},{3,1},{4,6},{5,7},{6,4},{7,5},{8,10},{9,11},{10,... | collective-permute-start | bytes 835592 | tf_op jit(solution)/shard_map/ppermute | solution.py:35
  24.3 1.5 %collective-permute-start.13 = (bf16[272,512]{1,0:T(8,128)(2,1)}, bf16[272,512]{1,0:T(8,128)(2,1)S(1)}, u32[]{:S(2)}, u32[]{:S(2)}) collective-permute-start(bf16[272,512]{1,0:T(8,128)(2,1)} %get-tuple-element.47.refs_8_.refs_4_), channel_id=1, source_target_pairs={{0,1},{1,0},{2,3},{3,2},{4,5},{5,4},{6,7},{7,6},{8,9},{9,8},{10,11... | collective-permute-start | bytes 835592 | tf_op jit(solution)/shard_map/ppermute | solution.py:35
  25.8 2.0 %collective-permute-done.11.refs_6_ = bf16[192,512]{1,0:T(8,128)(2,1)S(1)} collective-permute-done((bf16[192,512]{1,0:T(8,128)(2,1)S(1)}, bf16[192,512]{1,0:T(8,128)(2,1)S(1)}, u32[]{:S(2)}, u32[]{:S(2)}) %collective-permute-start.11) | collective-permute-done | bytes 196640 | tf_op jit(solution)/shard_map/ppermute | solution.py:35
  27.8 1.5 %collective-permute-start.5 = (bf16[192,512]{1,0:T(8,128)(2,1)S(1)}, bf16[192,512]{1,0:T(8,128)(2,1)S(1)}, u32[]{:S(2)}, u32[]{:S(2)}) collective-permute-start(bf16[192,512]{1,0:T(8,128)(2,1)S(1)} %collective-permute-done.3.refs_1_), channel_id=1, source_target_pairs={{0,2},{1,3},{2,0},{3,1},{4,6},{5,7},{6,4},{7,5},{8,10},{9,11},{10,... | collective-permute-start | bytes 589832 | tf_op jit(solution)/shard_map/ppermute | solution.py:35
  29.3 1.5 %collective-permute-start.12 = (bf16[192,512]{1,0:T(8,128)(2,1)S(1)}, bf16[192,512]{1,0:T(8,128)(2,1)S(1)}, u32[]{:S(2)}, u32[]{:S(2)}) collective-permute-start(bf16[192,512]{1,0:T(8,128)(2,1)S(1)} %collective-permute-done.11.refs_6_), channel_id=1, source_target_pairs={{0,1},{1,0},{2,3},{3,2},{4,5},{5,4},{6,7},{7,6},{8,9},{9,8},{10,11... | collective-permute-start | bytes 589832 | tf_op jit(solution)/shard_map/ppermute | solution.py:35
  30.8 1.6 %copy-done = bf16[512,2048]{1,0:T(8,128)(2,1)S(1)} copy-done((bf16[512,2048]{1,0:T(8,128)(2,1)S(1)}, bf16[512,2048]{1,0:T(8,128)(2,1)}, u32[]{:S(2)}) %copy-start) | copy-done | bytes 2097176
  32.4 1.0 copy-done.2
  34.8 4.2 %collective-permute-done.14.refs_10_.refs_6_ = bf16[272,512]{1,0:T(8,128)(2,1)S(1)} collective-permute-done((bf16[272,512]{1,0:T(8,128)(2,1)}, bf16[272,512]{1,0:T(8,128)(2,1)S(1)}, u32[]{:S(2)}, u32[]{:S(2)}) %collective-permute-start.14) | collective-permute-done | bytes 278560 | tf_op jit(solution)/shard_map/ppermute | solution.py:35
  39.0 1.6 %collective-permute-done.13.refs_9_.refs_5_ = bf16[272,512]{1,0:T(8,128)(2,1)S(1)} collective-permute-done((bf16[272,512]{1,0:T(8,128)(2,1)}, bf16[272,512]{1,0:T(8,128)(2,1)S(1)}, u32[]{:S(2)}, u32[]{:S(2)}) %collective-permute-start.13) | collective-permute-done | bytes 278560 | tf_op jit(solution)/shard_map/ppermute | solution.py:35
  40.5 1.8 %collective-permute-done.5.refs_3_ = bf16[192,512]{1,0:T(8,128)(2,1)S(1)} collective-permute-done((bf16[192,512]{1,0:T(8,128)(2,1)S(1)}, bf16[192,512]{1,0:T(8,128)(2,1)S(1)}, u32[]{:S(2)}, u32[]{:S(2)}) %collective-permute-start.5) | collective-permute-done | bytes 196640 | tf_op jit(solution)/shard_map/ppermute | solution.py:35
  42.4 1.3 %collective-permute-done.12.refs_7_ = bf16[192,512]{1,0:T(8,128)(2,1)S(1)} collective-permute-done((bf16[192,512]{1,0:T(8,128)(2,1)S(1)}, bf16[192,512]{1,0:T(8,128)(2,1)S(1)}, u32[]{:S(2)}, u32[]{:S(2)}) %collective-permute-start.12) | collective-permute-done | bytes 196640 | tf_op jit(solution)/shard_map/ppermute | solution.py:35
  43.7 7.2 %shard_map.104 = (bf16[256,512]{1,0:T(8,128)(2,1)S(1)}, bf16[512,1024]{1,0:T(8,128)(2,1)S(1)}, f32[1024,512]{1,0:T(8,128)S(1)}, bf16[1024,512]{1,0:T(8,128)(2,1)...) custom-call(bf16[192,512]{1,0:T(8,128)(2,1)S(1)} %constant_dynamic-update-slice_fusion.refs_0_, ...), custom_call_target="tpu_custom_call" | custom-call | flops 536870912 | bytes 8867840 | tf_op jit(solution)/shard_map/pallas_call | solution.py:325
  50.9 1.5 %collective-permute-start.18 = (f32[4,8,128]{2,1,0:T(8,128)S(1)}, f32[4,8,128]{2,1,0:T(8,128)S(1)}, u32[]{:S(2)}, u32[]{:S(2)}) collective-permute-start(f32[4,8,128]{2,1,0:T(8,128)S(1)} %get-tuple-element.51.refs_0_), channel_id=1, source_target_pairs={{0,3},{1,2},{2,1},{3,0},{4,7},{5,6},{6,5},{7,4},{8,11},{9,10},{10,... | collective-permute-start | bytes 49160 | tf_op jit(solution)/shard_map/ppermute | solution.py:35
  52.3 1.5 %collective-permute-start.17 = (f32[4,8,128]{2,1,0:T(8,128)S(1)}, f32[4,8,128]{2,1,0:T(8,128)S(1)}, u32[]{:S(2)}, u32[]{:S(2)}) collective-permute-start(f32[4,8,128]{2,1,0:T(8,128)S(1)} %get-tuple-element.51.refs_0_), channel_id=1, source_target_pairs={{0,2},{1,3},{2,0},{3,1},{4,6},{5,7},{6,4},{7,5},{8,10},{9,11},{10,... | collective-permute-start | bytes 49160 | tf_op jit(solution)/shard_map/ppermute | solution.py:35
  54.4 1.1 collective-permute-done.18.refs_3_
  56.1 1.5 %collective-permute-done.16.refs_1_ = f32[4,8,128]{2,1,0:T(8,128)S(1)} collective-permute-done((f32[4,8,128]{2,1,0:T(8,128)S(1)}, f32[4,8,128]{2,1,0:T(8,128)S(1)}, u32[]{:S(2)}, u32[]{:S(2)}) %collective-permute-start.16) | collective-permute-done | bytes 16416 | tf_op jit(solution)/shard_map/ppermute | solution.py:35
  57.6 7.7 %shard_map.105 = (bf16[4,160,128]{2,1,0:T(8,128)(2,1)S(1)}, bf16[4,160,128]{2,1,0:T(8,128)(2,1)S(1)}, bf16[4,160,128]{2,1,0:T(8,128)(2,1)S(1)}, bf16[4,160,128]{...) custom-call(f32[4,8,128]{2,1,0:T(8,128)S(1)} %get-tuple-element.51.r, ...), custom_call_target="tpu_custom_call" | custom-call | flops 1342177280 | bytes 8392704 | tf_op jit(solution)/shard_map/pallas_call | solution.py:464
  65.9 0.9 collective-permute-done.22.got_ref
  66.9 1.1 collective-permute-start.23
  68.0 1.0 collective-permute-start.30
  69.1 3.2 %collective-permute-done.23.got_ref = bf16[2,160,128]{2,1,0:T(8,128)(2,1)S(1)} collective-permute-done((bf16[2,160,128]{2,1,0:T(8,128)(2,1)S(1)}, bf16[2,160,128]{2,1,0:T(8,128)(2,1)S(1)}, u32[]{:S(2)}, u32[]{:S(2)}) %collective-permute-start.23) | collective-permute-done | bytes 81952 | tf_op jit(solution)/shard_map/ppermute | solution.py:35
  72.3 2.2 %collective-permute-start.24 = (bf16[2,160,128]{2,1,0:T(8,128)(2,1)S(1)}, bf16[2,160,128]{2,1,0:T(8,128)(2,1)S(1)}, u32[]{:S(2)}, u32[]{:S(2)}) collective-permute-start(bf16[2,160,128]{2,1,0:T(8,128)(2,1)S(1)} %shard_map.108.keep_ref), channel_id=1, source_target_pairs={{0,16},{4,20},{8,24},{12,28},{16,0},{20,4},{24,8},{28,12},{1,17},{... | collective-permute-start | bytes 245768 | tf_op jit(solution)/shard_map/ppermute | solution.py:35
  74.5 0.9 collective-permute-start.31
  75.4 5.2 %collective-permute-done.24.got_ref = bf16[2,160,128]{2,1,0:T(8,128)(2,1)S(1)} collective-permute-done((bf16[2,160,128]{2,1,0:T(8,128)(2,1)S(1)}, bf16[2,160,128]{2,1,0:T(8,128)(2,1)S(1)}, u32[]{:S(2)}, u32[]{:S(2)}) %collective-permute-start.24) | collective-permute-done | bytes 81952 | tf_op jit(solution)/shard_map/ppermute | solution.py:35
  80.7 0.8 collective-permute-done.31.got_ref
  81.5 1.3 %collective-permute-start.32 = (bf16[2,160,128]{2,1,0:T(8,128)(2,1)S(1)}, bf16[2,160,128]{2,1,0:T(8,128)(2,1)S(1)}, u32[]{:S(2)}, u32[]{:S(2)}) collective-permute-start(bf16[2,160,128]{2,1,0:T(8,128)(2,1)S(1)} %shard_map.112), channel_id=1, source_target_pairs={{0,8},{4,12},{8,0},{12,4},{16,24},{20,28},{24,16},{28,20},{1,9},{5... | collective-permute-start | bytes 245768 | tf_op jit(solution)/shard_map/ppermute | solution.py:35
  82.8 2.3 %collective-permute-done.25 = bf16[2,160,128]{2,1,0:T(8,128)(2,1)S(1)} collective-permute-done((bf16[2,160,128]{2,1,0:T(8,128)(2,1)S(1)}, bf16[2,160,128]{2,1,0:T(8,128)(2,1)S(1)}, u32[]{:S(2)}, u32[]{:S(2)}) %collective-permute-start.25) | collective-permute-done | bytes 81952 | tf_op jit(solution)/shard_map/ppermute | solution.py:35
  86.3 1.5 %collective-permute-start.34 = (bf16[4,160,128]{2,1,0:T(8,128)(2,1)S(1)}, bf16[4,160,128]{2,1,0:T(8,128)(2,1)S(1)}, u32[]{:S(2)}, u32[]{:S(2)}) collective-permute-start(bf16[4,160,128]{2,1,0:T(8,128)(2,1)S(1)} %pad_maximum_fusion.4.refs_4_), channel_id=1, source_target_pairs={{0,1},{1,0},{2,3},{3,2},{4,5},{5,4},{6,7},{7,6},{8,9},{9,8},{10,11... | collective-permute-start | bytes 491528 | tf_op jit(solution)/shard_map/ppermute | solution.py:35
  87.9 1.5 %collective-permute-start.33 = (bf16[4,160,128]{2,1,0:T(8,128)(2,1)S(1)}, bf16[4,160,128]{2,1,0:T(8,128)(2,1)S(1)}, u32[]{:S(2)}, u32[]{:S(2)}) collective-permute-start(bf16[4,160,128]{2,1,0:T(8,128)(2,1)S(1)} %pad_maximum_fusion.4.refs_4_), channel_id=1, source_target_pairs={{0,2},{1,3},{2,0},{3,1},{4,6},{5,7},{6,4},{7,5},{8,10},{9,11},{10,... | collective-permute-start | bytes 491528 | tf_op jit(solution)/shard_map/ppermute | solution.py:35
  90.5 2.3 %collective-permute-done.26.refs_1_ = bf16[4,160,128]{2,1,0:T(8,128)(2,1)S(1)} collective-permute-done((bf16[4,160,128]{2,1,0:T(8,128)(2,1)S(1)}, bf16[4,160,128]{2,1,0:T(8,128)(2,1)S(1)}, u32[]{:S(2)}, u32[]{:S(2)}) %collective-permute-start.26) | collective-permute-done | bytes 163872 | tf_op jit(solution)/shard_map/ppermute | solution.py:35
  92.8 2.3 %collective-permute-done.34.refs_6_ = bf16[4,160,128]{2,1,0:T(8,128)(2,1)S(1)} collective-permute-done((bf16[4,160,128]{2,1,0:T(8,128)(2,1)S(1)}, bf16[4,160,128]{2,1,0:T(8,128)(2,1)S(1)}, u32[]{:S(2)}, u32[]{:S(2)}) %collective-permute-start.34) | collective-permute-done | bytes 163872 | tf_op jit(solution)/shard_map/ppermute | solution.py:35
  95.8 1.3 %collective-permute-start.35 = (bf16[4,160,128]{2,1,0:T(8,128)(2,1)S(1)}, bf16[4,160,128]{2,1,0:T(8,128)(2,1)S(1)}, u32[]{:S(2)}, u32[]{:S(2)}) collective-permute-start(bf16[4,160,128]{2,1,0:T(8,128)(2,1)S(1)} %collective-permute-done.33.refs_5_), channel_id=1, source_target_pairs={{0,1},{1,0},{2,3},{3,2},{4,5},{5,4},{6,7},{7,6},{8,9},{9,8},{10,11... | collective-permute-start | bytes 491528 | tf_op jit(solution)/shard_map/ppermute | solution.py:35
  97.1 0.9 collective-permute-start.20
  98.0 4.4 %collective-permute-done.28.refs_3_ = bf16[4,160,128]{2,1,0:T(8,128)(2,1)S(1)} collective-permute-done((bf16[4,160,128]{2,1,0:T(8,128)(2,1)S(1)}, bf16[4,160,128]{2,1,0:T(8,128)(2,1)S(1)}, u32[]{:S(2)}, u32[]{:S(2)}) %collective-permute-start.28) | collective-permute-done | bytes 163872 | tf_op jit(solution)/shard_map/ppermute | solution.py:35
  102.4 1.2 collective-permute-start.21
  104.2 11.7 %collective-permute-done.20.refs_2_ = bf16[256,640]{1,0:T(8,128)(2,1)S(1)} collective-permute-done((bf16[256,640]{1,0:T(8,128)(2,1)S(1)}, bf16[256,640]{1,0:T(8,128)(2,1)S(1)}, u32[]{:S(2)}, u32[]{:S(2)}) %collective-permute-start.20) | collective-permute-done | bytes 327712 | tf_op jit(solution)/shard_map/ppermute | solution.py:35
  115.9 2.4 %shard_map.106 = (bf16[256,512]{1,0:T(8,128)(2,1)}, bf16[256,512]{1,0:T(8,128)(2,1)}) custom-call(bf16[256,640]{1,0:T(8,128)(2,1)S(1)} %get-tuple-element.57.refs_0_, bf16[256,640]{1,0:T(8,128)(2,1)S(1)} %collective-permute-done.19.refs_1_, bf16[256,640]{1,0:T(8,128)(2,1)S(1)} %collective-permute-done.20.refs_2_, ...), custom_call_target="tpu_custom_call" | custom-call | flops 671088640 | bytes 4980736 | tf_op jit(solution)/shard_map/pallas_call | solution.py:544
  118.4 3.1 %shard_map.113 = (f32[512,2048]{1,0:T(8,128)}, f32[512,512]{1,0:T(8,128)}) custom-call(bf16[4,160,128]{2,1,0:T(8,128)(2,1)S(1)} %pad_maximum_fusion.3.refs_0_, bf16[4,160,128]{2,1,0:T(8,128)(2,1)S(1)} %collective-permute-done.26.refs_1_, bf16[4,160,128]{2,1,0:T(8,128)(2,1)S(1)} %collective-permute-done.27.refs_2_, ...), custom_call_target="tpu_custom_call" | custom-call | flops 2621440 | bytes 7864320 | tf_op jit(solution)/shard_map/pallas_call | solution.py:582
  (69 shorter events, 8.2 us)
Async XLA Ops:
  2.9 40.7 %copy-start.4 = (bf16[272,512]{1,0:T(8,128)(2,1)S(1)}, bf16[272,512]{1,0:T(8,128)(2,1)}, u32[]{:S(2)}) copy-start(bf16[272,512]{1,0:T(8,128)(2,1)} %get-tuple-element.47.refs_8_.refs_4_) | copy-start | bytes 835588
  2.9 6.8 %collective-permute-start = (bf16[48,512]{1,0:T(8,128)(2,1)}, bf16[48,512]{1,0:T(8,128)(2,1)S(1)}, u32[]{:S(2)}, u32[]{:S(2)}) collective-permute-start(bf16[48,512]{1,0:T(8,128)(2,1)} %get-tuple-element.40), channel_id=1, source_target_pairs={{0,4},{4,0},{8,12},{12,8},{16,20},{20,16},{24,28},{28,24},{1,5},{5... | collective-permute-start | bytes 147464 | tf_op jit(solution)/shard_map/ppermute | solution.py:35
  3.5 9.9 %collective-permute-start.1 = (bf16[48,512]{1,0:T(8,128)(2,1)}, bf16[48,512]{1,0:T(8,128)(2,1)S(1)}, u32[]{:S(2)}, u32[]{:S(2)}) collective-permute-start(bf16[48,512]{1,0:T(8,128)(2,1)} %get-tuple-element.41), channel_id=1, source_target_pairs={{0,8},{4,12},{8,0},{12,4},{16,24},{20,28},{24,16},{28,20},{1,9},{5... | collective-permute-start | bytes 147464 | tf_op jit(solution)/shard_map/ppermute | solution.py:35
  6.1 7.4 %collective-permute-start.2 = (bf16[48,512]{1,0:T(8,128)(2,1)}, bf16[48,512]{1,0:T(8,128)(2,1)S(1)}, u32[]{:S(2)}, u32[]{:S(2)}) collective-permute-start(bf16[48,512]{1,0:T(8,128)(2,1)} %get-tuple-element.42), channel_id=1, source_target_pairs={{0,12},{4,8},{8,4},{12,0},{16,28},{20,24},{24,20},{28,16},{1,13},{... | collective-permute-start | bytes 147464 | tf_op jit(solution)/shard_map/ppermute | solution.py:35
  6.2 8.9 %collective-permute-start.6 = (bf16[48,512]{1,0:T(8,128)(2,1)}, bf16[48,512]{1,0:T(8,128)(2,1)S(1)}, u32[]{:S(2)}, u32[]{:S(2)}) collective-permute-start(bf16[48,512]{1,0:T(8,128)(2,1)} %get-tuple-element.43), channel_id=1, source_target_pairs={{0,16},{4,20},{8,24},{12,28},{16,0},{20,4},{24,8},{28,12},{1,17},{... | collective-permute-start | bytes 147464 | tf_op jit(solution)/shard_map/ppermute | solution.py:35
  8.9 7.7 %collective-permute-start.7 = (bf16[48,512]{1,0:T(8,128)(2,1)}, bf16[48,512]{1,0:T(8,128)(2,1)S(1)}, u32[]{:S(2)}, u32[]{:S(2)}) collective-permute-start(bf16[48,512]{1,0:T(8,128)(2,1)} %get-tuple-element.44), channel_id=1, source_target_pairs={{0,20},{4,16},{8,28},{12,24},{16,4},{20,0},{24,12},{28,8},{1,21},{... | collective-permute-start | bytes 147464 | tf_op jit(solution)/shard_map/ppermute | solution.py:35
  9.8 6.9 %collective-permute-start.8 = (bf16[48,512]{1,0:T(8,128)(2,1)}, bf16[48,512]{1,0:T(8,128)(2,1)S(1)}, u32[]{:S(2)}, u32[]{:S(2)}) collective-permute-start(bf16[48,512]{1,0:T(8,128)(2,1)} %get-tuple-element.45), channel_id=1, source_target_pairs={{0,24},{4,28},{8,16},{12,20},{16,8},{20,12},{24,0},{28,4},{1,25},{... | collective-permute-start | bytes 147464 | tf_op jit(solution)/shard_map/ppermute | solution.py:35
  13.4 5.9 %collective-permute-start.9 = (bf16[48,512]{1,0:T(8,128)(2,1)}, bf16[48,512]{1,0:T(8,128)(2,1)S(1)}, u32[]{:S(2)}, u32[]{:S(2)}) collective-permute-start(bf16[48,512]{1,0:T(8,128)(2,1)} %get-tuple-element.46), channel_id=1, source_target_pairs={{0,28},{4,24},{8,20},{12,16},{16,12},{20,8},{24,4},{28,0},{1,29},{... | collective-permute-start | bytes 147464 | tf_op jit(solution)/shard_map/ppermute | solution.py:35
  13.5 9.2 %collective-permute-start.4 = (bf16[192,512]{1,0:T(8,128)(2,1)S(1)}, bf16[192,512]{1,0:T(8,128)(2,1)S(1)}, u32[]{:S(2)}, u32[]{:S(2)}) collective-permute-start(bf16[192,512]{1,0:T(8,128)(2,1)S(1)} %constant_dynamic-update-slice_fusion.refs_0_), channel_id=1, source_target_pairs={{0,2},{1,3},{2,0},{3,1},{4,6},{5,7},{6,4},{7,5},{8,10},{9,11},{10,... | collective-permute-start | bytes 589832 | tf_op jit(solution)/shard_map/ppermute | solution.py:35
  15.1 9.2 %collective-permute-start.3 = (bf16[192,512]{1,0:T(8,128)(2,1)S(1)}, bf16[192,512]{1,0:T(8,128)(2,1)S(1)}, u32[]{:S(2)}, u32[]{:S(2)}) collective-permute-start(bf16[192,512]{1,0:T(8,128)(2,1)S(1)} %constant_dynamic-update-slice_fusion.refs_0_), channel_id=1, source_target_pairs={{0,1},{1,0},{2,3},{3,2},{4,5},{5,4},{6,7},{7,6},{8,9},{9,8},{10,11... | collective-permute-start | bytes 589832 | tf_op jit(solution)/shard_map/ppermute | solution.py:35
  19.3 8.5 %collective-permute-start.11 = (bf16[192,512]{1,0:T(8,128)(2,1)S(1)}, bf16[192,512]{1,0:T(8,128)(2,1)S(1)}, u32[]{:S(2)}, u32[]{:S(2)}) collective-permute-start(bf16[192,512]{1,0:T(8,128)(2,1)S(1)} %constant_dynamic-update-slice_fusion.4.refs_4_), channel_id=1, source_target_pairs={{0,2},{1,3},{2,0},{3,1},{4,6},{5,7},{6,4},{7,5},{8,10},{9,11},{10,... | collective-permute-start | bytes 589832 | tf_op jit(solution)/shard_map/ppermute | solution.py:35
  20.8 8.5 %collective-permute-start.10 = (bf16[192,512]{1,0:T(8,128)(2,1)S(1)}, bf16[192,512]{1,0:T(8,128)(2,1)S(1)}, u32[]{:S(2)}, u32[]{:S(2)}) collective-permute-start(bf16[192,512]{1,0:T(8,128)(2,1)S(1)} %constant_dynamic-update-slice_fusion.4.refs_4_), channel_id=1, source_target_pairs={{0,1},{1,0},{2,3},{3,2},{4,5},{5,4},{6,7},{7,6},{8,9},{9,8},{10,11... | collective-permute-start | bytes 589832 | tf_op jit(solution)/shard_map/ppermute | solution.py:35
  22.3 12.5 %collective-permute-start.15 = (bf16[272,512]{1,0:T(8,128)(2,1)}, bf16[272,512]{1,0:T(8,128)(2,1)S(1)}, u32[]{:S(2)}, u32[]{:S(2)}) collective-permute-start(bf16[272,512]{1,0:T(8,128)(2,1)} %get-tuple-element.47.refs_8_.refs_4_), channel_id=1, source_target_pairs={{0,3},{1,2},{2,1},{3,0},{4,7},{5,6},{6,5},{7,4},{8,11},{9,10},{10,... | collective-permute-start | bytes 835592 | tf_op jit(solution)/shard_map/ppermute | solution.py:35
  22.8 16.2 %collective-permute-start.14 = (bf16[272,512]{1,0:T(8,128)(2,1)}, bf16[272,512]{1,0:T(8,128)(2,1)S(1)}, u32[]{:S(2)}, u32[]{:S(2)}) collective-permute-start(bf16[272,512]{1,0:T(8,128)(2,1)} %get-tuple-element.47.refs_8_.refs_4_), channel_id=1, source_target_pairs={{0,2},{1,3},{2,0},{3,1},{4,6},{5,7},{6,4},{7,5},{8,10},{9,11},{10,... | collective-permute-start | bytes 835592 | tf_op jit(solution)/shard_map/ppermute | solution.py:35
  24.3 16.3 %collective-permute-start.13 = (bf16[272,512]{1,0:T(8,128)(2,1)}, bf16[272,512]{1,0:T(8,128)(2,1)S(1)}, u32[]{:S(2)}, u32[]{:S(2)}) collective-permute-start(bf16[272,512]{1,0:T(8,128)(2,1)} %get-tuple-element.47.refs_8_.refs_4_), channel_id=1, source_target_pairs={{0,1},{1,0},{2,3},{3,2},{4,5},{5,4},{6,7},{7,6},{8,9},{9,8},{10,11... | collective-permute-start | bytes 835592 | tf_op jit(solution)/shard_map/ppermute | solution.py:35
  27.8 14.6 %collective-permute-start.5 = (bf16[192,512]{1,0:T(8,128)(2,1)S(1)}, bf16[192,512]{1,0:T(8,128)(2,1)S(1)}, u32[]{:S(2)}, u32[]{:S(2)}) collective-permute-start(bf16[192,512]{1,0:T(8,128)(2,1)S(1)} %collective-permute-done.3.refs_1_), channel_id=1, source_target_pairs={{0,2},{1,3},{2,0},{3,1},{4,6},{5,7},{6,4},{7,5},{8,10},{9,11},{10,... | collective-permute-start | bytes 589832 | tf_op jit(solution)/shard_map/ppermute | solution.py:35
  29.3 14.4 %collective-permute-start.12 = (bf16[192,512]{1,0:T(8,128)(2,1)S(1)}, bf16[192,512]{1,0:T(8,128)(2,1)S(1)}, u32[]{:S(2)}, u32[]{:S(2)}) collective-permute-start(bf16[192,512]{1,0:T(8,128)(2,1)S(1)} %collective-permute-done.11.refs_6_), channel_id=1, source_target_pairs={{0,1},{1,0},{2,3},{3,2},{4,5},{5,4},{6,7},{7,6},{8,9},{9,8},{10,11... | collective-permute-start | bytes 589832 | tf_op jit(solution)/shard_map/ppermute | solution.py:35
  30.8 1.6 %copy-start = (bf16[512,2048]{1,0:T(8,128)(2,1)S(1)}, bf16[512,2048]{1,0:T(8,128)(2,1)}, u32[]{:S(2)}) copy-start(bf16[512,2048]{1,0:T(8,128)(2,1)} %refs_6_.1) | copy-start | bytes 6291460
  32.4 1.0 copy-start.2
  33.4 0.7 copy-start.6
  50.9 4.7 %collective-permute-start.18 = (f32[4,8,128]{2,1,0:T(8,128)S(1)}, f32[4,8,128]{2,1,0:T(8,128)S(1)}, u32[]{:S(2)}, u32[]{:S(2)}) collective-permute-start(f32[4,8,128]{2,1,0:T(8,128)S(1)} %get-tuple-element.51.refs_0_), channel_id=1, source_target_pairs={{0,3},{1,2},{2,1},{3,0},{4,7},{5,6},{6,5},{7,4},{8,11},{9,10},{10,... | collective-permute-start | bytes 49160 | tf_op jit(solution)/shard_map/ppermute | solution.py:35
  52.3 3.7 %collective-permute-start.17 = (f32[4,8,128]{2,1,0:T(8,128)S(1)}, f32[4,8,128]{2,1,0:T(8,128)S(1)}, u32[]{:S(2)}, u32[]{:S(2)}) collective-permute-start(f32[4,8,128]{2,1,0:T(8,128)S(1)} %get-tuple-element.51.refs_0_), channel_id=1, source_target_pairs={{0,2},{1,3},{2,0},{3,1},{4,6},{5,7},{6,4},{7,5},{8,10},{9,11},{10,... | collective-permute-start | bytes 49160 | tf_op jit(solution)/shard_map/ppermute | solution.py:35
  53.9 3.7 %collective-permute-start.16 = (f32[4,8,128]{2,1,0:T(8,128)S(1)}, f32[4,8,128]{2,1,0:T(8,128)S(1)}, u32[]{:S(2)}, u32[]{:S(2)}) collective-permute-start(f32[4,8,128]{2,1,0:T(8,128)S(1)} %get-tuple-element.51.refs_0_), channel_id=1, source_target_pairs={{0,1},{1,0},{2,3},{3,2},{4,5},{5,4},{6,7},{7,6},{8,9},{9,8},{10,11... | collective-permute-start | bytes 49160 | tf_op jit(solution)/shard_map/ppermute | solution.py:35
  65.3 1.5 %collective-permute-start.22 = (bf16[4,160,128]{2,1,0:T(8,128)(2,1)S(1)}, bf16[4,160,128]{2,1,0:T(8,128)(2,1)S(1)}, u32[]{:S(2)}, u32[]{:S(2)}) collective-permute-start(bf16[4,160,128]{2,1,0:T(8,128)(2,1)S(1)} %get-tuple-element.65), channel_id=1, source_target_pairs={{0,4},{4,0},{8,12},{12,8},{16,20},{20,16},{24,28},{28,24},{1,5},{5... | collective-permute-start | bytes 491528 | tf_op jit(solution)/shard_map/ppermute | solution.py:35
  65.4 2.6 %collective-permute-start.29 = (bf16[4,160,128]{2,1,0:T(8,128)(2,1)S(1)}, bf16[4,160,128]{2,1,0:T(8,128)(2,1)S(1)}, u32[]{:S(2)}, u32[]{:S(2)}) collective-permute-start(bf16[4,160,128]{2,1,0:T(8,128)(2,1)S(1)} %get-tuple-element.69), channel_id=1, source_target_pairs={{0,4},{4,0},{8,12},{12,8},{16,20},{20,16},{24,28},{28,24},{1,5},{5... | collective-permute-start | bytes 491528 | tf_op jit(solution)/shard_map/ppermute | solution.py:35
  66.9 5.4 %collective-permute-start.23 = (bf16[2,160,128]{2,1,0:T(8,128)(2,1)S(1)}, bf16[2,160,128]{2,1,0:T(8,128)(2,1)S(1)}, u32[]{:S(2)}, u32[]{:S(2)}) collective-permute-start(bf16[2,160,128]{2,1,0:T(8,128)(2,1)S(1)} %get-tuple-element.67), channel_id=1, source_target_pairs={{0,8},{4,12},{8,0},{12,4},{16,24},{20,28},{24,16},{28,20},{1,9},{5... | collective-permute-start | bytes 245768 | tf_op jit(solution)/shard_map/ppermute | solution.py:35
  68.0 6.4 %collective-permute-start.30 = (bf16[2,160,128]{2,1,0:T(8,128)(2,1)S(1)}, bf16[2,160,128]{2,1,0:T(8,128)(2,1)S(1)}, u32[]{:S(2)}, u32[]{:S(2)}) collective-permute-start(bf16[2,160,128]{2,1,0:T(8,128)(2,1)S(1)} %get-tuple-element.71), channel_id=1, source_target_pairs={{0,8},{4,12},{8,0},{12,4},{16,24},{20,28},{24,16},{28,20},{1,9},{5... | collective-permute-start | bytes 245768 | tf_op jit(solution)/shard_map/ppermute | solution.py:35
  72.2 43.7 %copy-start.1 = (bf16[512,2048]{1,0:T(8,128)(2,1)S(1)}, bf16[512,2048]{1,0:T(8,128)(2,1)}, u32[]{:S(2)}) copy-start(bf16[512,2048]{1,0:T(8,128)(2,1)} %refs_6_.1) | copy-start | bytes 6291460
  72.2 43.7 %copy-start.3 = (bf16[512,512]{1,0:T(8,128)(2,1)S(1)}, bf16[512,512]{1,0:T(8,128)(2,1)}, u32[]{:S(2)}) copy-start(bf16[512,512]{1,0:T(8,128)(2,1)} %refs_7_.1) | copy-start | bytes 1572868
  72.2 43.7 %copy-start.5 = (bf16[256,512]{1,0:T(8,128)(2,1)S(1)}, bf16[256,512]{1,0:T(8,128)(2,1)}, u32[]{:S(2)}) copy-start(bf16[256,512]{1,0:T(8,128)(2,1)} %refs_5_.1) | copy-start | bytes 786436
  72.3 8.3 %collective-permute-start.24 = (bf16[2,160,128]{2,1,0:T(8,128)(2,1)S(1)}, bf16[2,160,128]{2,1,0:T(8,128)(2,1)S(1)}, u32[]{:S(2)}, u32[]{:S(2)}) collective-permute-start(bf16[2,160,128]{2,1,0:T(8,128)(2,1)S(1)} %shard_map.108.keep_ref), channel_id=1, source_target_pairs={{0,16},{4,20},{8,24},{12,28},{16,0},{20,4},{24,8},{28,12},{1,17},{... | collective-permute-start | bytes 245768 | tf_op jit(solution)/shard_map/ppermute | solution.py:35
  74.5 7.0 %collective-permute-start.31 = (bf16[2,160,128]{2,1,0:T(8,128)(2,1)S(1)}, bf16[2,160,128]{2,1,0:T(8,128)(2,1)S(1)}, u32[]{:S(2)}, u32[]{:S(2)}) collective-permute-start(bf16[2,160,128]{2,1,0:T(8,128)(2,1)S(1)} %shard_map.111.keep_ref), channel_id=1, source_target_pairs={{0,16},{4,20},{8,24},{12,28},{16,0},{20,4},{24,8},{28,12},{1,17},{... | collective-permute-start | bytes 245768 | tf_op jit(solution)/shard_map/ppermute | solution.py:35
  80.6 4.5 %collective-permute-start.25 = (bf16[2,160,128]{2,1,0:T(8,128)(2,1)S(1)}, bf16[2,160,128]{2,1,0:T(8,128)(2,1)S(1)}, u32[]{:S(2)}, u32[]{:S(2)}) collective-permute-start(bf16[2,160,128]{2,1,0:T(8,128)(2,1)S(1)} %shard_map.109), channel_id=1, source_target_pairs={{0,8},{4,12},{8,0},{12,4},{16,24},{20,28},{24,16},{28,20},{1,9},{5... | collective-permute-start | bytes 245768 | tf_op jit(solution)/shard_map/ppermute | solution.py:35
  81.5 4.8 %collective-permute-start.32 = (bf16[2,160,128]{2,1,0:T(8,128)(2,1)S(1)}, bf16[2,160,128]{2,1,0:T(8,128)(2,1)S(1)}, u32[]{:S(2)}, u32[]{:S(2)}) collective-permute-start(bf16[2,160,128]{2,1,0:T(8,128)(2,1)S(1)} %shard_map.112), channel_id=1, source_target_pairs={{0,8},{4,12},{8,0},{12,4},{16,24},{20,28},{24,16},{28,20},{1,9},{5... | collective-permute-start | bytes 245768 | tf_op jit(solution)/shard_map/ppermute | solution.py:35
  85.2 5.4 %collective-permute-start.27 = (bf16[4,160,128]{2,1,0:T(8,128)(2,1)S(1)}, bf16[4,160,128]{2,1,0:T(8,128)(2,1)S(1)}, u32[]{:S(2)}, u32[]{:S(2)}) collective-permute-start(bf16[4,160,128]{2,1,0:T(8,128)(2,1)S(1)} %pad_maximum_fusion.3.refs_0_), channel_id=1, source_target_pairs={{0,2},{1,3},{2,0},{3,1},{4,6},{5,7},{6,4},{7,5},{8,10},{9,11},{10,... | collective-permute-start | bytes 491528 | tf_op jit(solution)/shard_map/ppermute | solution.py:35
  85.8 7.1 %collective-permute-start.26 = (bf16[4,160,128]{2,1,0:T(8,128)(2,1)S(1)}, bf16[4,160,128]{2,1,0:T(8,128)(2,1)S(1)}, u32[]{:S(2)}, u32[]{:S(2)}) collective-permute-start(bf16[4,160,128]{2,1,0:T(8,128)(2,1)S(1)} %pad_maximum_fusion.3.refs_0_), channel_id=1, source_target_pairs={{0,1},{1,0},{2,3},{3,2},{4,5},{5,4},{6,7},{7,6},{8,9},{9,8},{10,11... | collective-permute-start | bytes 491528 | tf_op jit(solution)/shard_map/ppermute | solution.py:35
  86.3 8.8 %collective-permute-start.34 = (bf16[4,160,128]{2,1,0:T(8,128)(2,1)S(1)}, bf16[4,160,128]{2,1,0:T(8,128)(2,1)S(1)}, u32[]{:S(2)}, u32[]{:S(2)}) collective-permute-start(bf16[4,160,128]{2,1,0:T(8,128)(2,1)S(1)} %pad_maximum_fusion.4.refs_4_), channel_id=1, source_target_pairs={{0,1},{1,0},{2,3},{3,2},{4,5},{5,4},{6,7},{7,6},{8,9},{9,8},{10,11... | collective-permute-start | bytes 491528 | tf_op jit(solution)/shard_map/ppermute | solution.py:35
  87.9 7.2 %collective-permute-start.33 = (bf16[4,160,128]{2,1,0:T(8,128)(2,1)S(1)}, bf16[4,160,128]{2,1,0:T(8,128)(2,1)S(1)}, u32[]{:S(2)}, u32[]{:S(2)}) collective-permute-start(bf16[4,160,128]{2,1,0:T(8,128)(2,1)S(1)} %pad_maximum_fusion.4.refs_4_), channel_id=1, source_target_pairs={{0,2},{1,3},{2,0},{3,1},{4,6},{5,7},{6,4},{7,5},{8,10},{9,11},{10,... | collective-permute-start | bytes 491528 | tf_op jit(solution)/shard_map/ppermute | solution.py:35
  89.4 14.3 %collective-permute-start.19 = (bf16[256,640]{1,0:T(8,128)(2,1)S(1)}, bf16[256,640]{1,0:T(8,128)(2,1)S(1)}, u32[]{:S(2)}, u32[]{:S(2)}) collective-permute-start(bf16[256,640]{1,0:T(8,128)(2,1)S(1)} %get-tuple-element.58), channel_id=1, source_target_pairs={{0,1},{1,0},{2,3},{3,2},{4,5},{5,4},{6,7},{7,6},{8,9},{9,8},{10,11... | collective-permute-start | bytes 983048 | tf_op jit(solution)/shard_map/ppermute | solution.py:35
  95.2 23.2 %collective-permute-start.37 = (bf16[16,160,128]{2,1,0:T(8,128)(2,1)S(1)}, bf16[16,160,128]{2,1,0:T(8,128)(2,1)S(1)}, u32[]{:S(2)}, u32[]{:S(2)}) collective-permute-start(bf16[16,160,128]{2,1,0:T(8,128)(2,1)S(1)} %pad_maximum_fusion), channel_id=1, source_target_pairs={{0,4},{4,0},{8,12},{12,8},{16,20},{20,16},{24,28},{28,24},{1,5},{5... | collective-permute-start | bytes 1966088 | tf_op jit(solution)/shard_map/ppermute | solution.py:35
  95.3 7.1 %collective-permute-start.28 = (bf16[4,160,128]{2,1,0:T(8,128)(2,1)S(1)}, bf16[4,160,128]{2,1,0:T(8,128)(2,1)S(1)}, u32[]{:S(2)}, u32[]{:S(2)}) collective-permute-start(bf16[4,160,128]{2,1,0:T(8,128)(2,1)S(1)} %collective-permute-done.26.refs_1_), channel_id=1, source_target_pairs={{0,2},{1,3},{2,0},{3,1},{4,6},{5,7},{6,4},{7,5},{8,10},{9,11},{10,... | collective-permute-start | bytes 491528 | tf_op jit(solution)/shard_map/ppermute | solution.py:35
  95.8 7.8 %collective-permute-start.35 = (bf16[4,160,128]{2,1,0:T(8,128)(2,1)S(1)}, bf16[4,160,128]{2,1,0:T(8,128)(2,1)S(1)}, u32[]{:S(2)}, u32[]{:S(2)}) collective-permute-start(bf16[4,160,128]{2,1,0:T(8,128)(2,1)S(1)} %collective-permute-done.33.refs_5_), channel_id=1, source_target_pairs={{0,1},{1,0},{2,3},{3,2},{4,5},{5,4},{6,7},{7,6},{8,9},{9,8},{10,11... | collective-permute-start | bytes 491528 | tf_op jit(solution)/shard_map/ppermute | solution.py:35
  97.1 18.8 %collective-permute-start.20 = (bf16[256,640]{1,0:T(8,128)(2,1)S(1)}, bf16[256,640]{1,0:T(8,128)(2,1)S(1)}, u32[]{:S(2)}, u32[]{:S(2)}) collective-permute-start(bf16[256,640]{1,0:T(8,128)(2,1)S(1)} %get-tuple-element.59), channel_id=1, source_target_pairs={{0,2},{1,3},{2,0},{3,1},{4,6},{5,7},{6,4},{7,5},{8,10},{9,11},{10,... | collective-permute-start | bytes 983048 | tf_op jit(solution)/shard_map/ppermute | solution.py:35
  102.4 13.5 %collective-permute-start.21 = (bf16[256,640]{1,0:T(8,128)(2,1)S(1)}, bf16[256,640]{1,0:T(8,128)(2,1)S(1)}, u32[]{:S(2)}, u32[]{:S(2)}) collective-permute-start(bf16[256,640]{1,0:T(8,128)(2,1)S(1)} %get-tuple-element.60), channel_id=1, source_target_pairs={{0,3},{1,2},{2,1},{3,0},{4,7},{5,6},{6,5},{7,4},{8,11},{9,10},{10,... | collective-permute-start | bytes 983048 | tf_op jit(solution)/shard_map/ppermute | solution.py:35
  103.6 14.8 %collective-permute-start.36 = (bf16[8,160,128]{2,1,0:T(8,128)(2,1)S(1)}, bf16[8,160,128]{2,1,0:T(8,128)(2,1)S(1)}, u32[]{:S(2)}, u32[]{:S(2)}) collective-permute-start(bf16[8,160,128]{2,1,0:T(8,128)(2,1)S(1)} %pad_maximum_fusion.1), channel_id=1, source_target_pairs={{0,4},{4,0},{8,12},{12,8},{16,20},{20,16},{24,28},{28,24},{1,5},{5... | collective-permute-start | bytes 983048 | tf_op jit(solution)/shard_map/ppermute | solution.py:35
  103.6 14.7 %collective-permute-start.38 = (bf16[8,160,128]{2,1,0:T(8,128)(2,1)S(1)}, bf16[8,160,128]{2,1,0:T(8,128)(2,1)S(1)}, u32[]{:S(2)}, u32[]{:S(2)}) collective-permute-start(bf16[8,160,128]{2,1,0:T(8,128)(2,1)S(1)} %pad_maximum_fusion.2), channel_id=1, source_target_pairs={{0,4},{4,0},{8,12},{12,8},{16,20},{20,16},{24,28},{28,24},{1,5},{5... | collective-permute-start | bytes 983048 | tf_op jit(solution)/shard_map/ppermute | solution.py:35
where the time goes:
time: 122 us; the launch traced here: 121 us
  waiting for transfers between devices  50.4 us (41%)
  starting transfers between devices  42.3 us (35%)
  Pallas kernels  23.6 us (19%)
  local copies, waits for them, and re-layouts  4.14 us (3%)
    ppermute x39, waiting for transfers between devices, swap(): lax.ppermute(values, axis, [(each, each ^ distance) for each in range(siz...  50.4 us
    ppermute x39, starting transfers between devices, swap(): lax.ppermute(values, axis, [(each, each ^ distance) for each in range(siz...  42.3 us
    pallas_call x1, Pallas kernels, local(): call(backward_kernel, bwd_outs, bwd_args, 10 * rows_all * rows_all * part...  7.74 us
    pallas_call x1, Pallas kernels, local(): call(forward_kernel, fwd_outs, fwd_args, 4 * rows_all * rows_all * part,...  7.21 us
    unnamed x20, local copies, waits for them, and re-layouts  4.13 us
    pallas_call x1, Pallas kernels, local(): call(finish_kernel, [shape((width, 4 * width), F32), shape((width, width)...  3.08 us
  transfers between devices with their start and end apart: 39, of which 19 were waited for; matrix products, arithmetic and copies ran while one was open for 1% of the time, Pallas kernels for 3%

commit v1 on v0

--- a/solution.py
+++ b/solution.py
@@ -233,8 +233,8 @@
         side_refs = (refs[:ctx], refs[ctx : 2 * ctx])
         cot_refs = refs[2 * ctx : 3 * ctx]
         begin_ref, own_weight_ref, out_own_ref = refs[3 * ctx : 3 * ctx + 3]
-        own_ref, norm_t_ref, pre_ref, proj_ref, att_ref, gg_ref, stat_ref = refs[3 * ctx + 3 : 3 * ctx + 10]
-        where_ref, rows_ref, query_ref, value_ref = refs[3 * ctx + 10 :]
+        own_ref, normed_ref, pre_ref, proj_ref, att_ref, gg_ref, stat_ref = refs[3 * ctx + 3 : 3 * ctx + 10]
+        where_ref, rows_ref, query_ref, value_ref, key_t_ref = refs[3 * ctx + 10 :]
         mine = lax.axis_index("ctx")
         out_own = out_own_ref[...]
         begins = jnp.transpose(begin_ref[...].astype(F32)).astype(jnp.int32)
@@ -260,13 +260,14 @@
                     total = total + nn_dot(picked, side_refs[side][rel][...])
             rows_ref[span, :] = total.astype(BF)
             normed = normalize(total)[0].astype(BF)
-            norm_t_ref[:, tile * TILE : (tile + 1) * TILE] = jnp.transpose(normed)
+            normed_ref[span, :] = normed
             pre = nn_dot(normed, own_weight_ref[...])
             pre_ref[span, :] = pre
             proj = silu(pre).astype(BF)
             proj_ref[span, :] = proj
             query = proj[:, 2 * part : 3 * part] * jnp.asarray(0.5 * scale, BF)
             value = proj[:, part : 2 * part]
+            key_t_ref[:, tile * TILE : (tile + 1) * TILE] = jnp.transpose(proj[:, 3 * part :])
             for head in range(heads):
                 query_ref[head, span, :] = jnp.where(masks[head], query, jnp.zeros_like(query))
                 value_ref[head, span, :] = jnp.where(masks[head], value, jnp.zeros_like(value))
@@ -285,9 +286,9 @@
                 allowed = key_pos >= begin
                 if key_at == at:
                     allowed = allowed & (key_pos <= query_pos)
-                key = proj_ref[key_span, 3 * part :]
+                key = key_t_ref[:, key_at * TILE : (key_at + 1) * TILE]
                 for head in range(heads):
-                    score = nt_dot(query_ref[head, span, :], key)
+                    score = nn_dot(query_ref[head, span, :], key)
                     weight = jnp.where(allowed, score + score * jnp.tanh(score), 0.0).astype(BF)
                     total = total + nn_dot(weight, value_ref[head, key_span, :])
             att_ref[span, :] = total
@@ -315,14 +316,14 @@
     )
     fwd_outs = [
         shape((own_count, width), BF),
-        shape((width, rows_all), BF),
+        shape((rows_all, width), BF),
         shape((rows_all, 4 * part), F32),
         shape((rows_all, 4 * part), BF),
         shape((rows_all, part), F32),
         shape((rows_all, part), F32),
         shape((4, blocks, half), F32),
     ]
-    own_rows, norm_t, pre, proj, attended, grad_gated, stats = call(
+    own_rows, normed_rows, pre, proj, attended, grad_gated, stats = call(
         forward_kernel, fwd_outs, fwd_args, 4 * rows_all * rows_all * part, limit=room
     )(
         scratch_shapes=[
@@ -330,11 +331,37 @@
             pltpu.VMEM((rows_all, width), BF),
             pltpu.VMEM((heads, rows_all, part), BF),
             pltpu.VMEM((heads, rows_all, part), BF),
+            pltpu.VMEM((part, rows_all), BF),
         ]
     )(*fwd_args)
 
     stats_of = direct([stats] * ctx, "ctx")
 
+    def between_kernel(normed_ref, pre_ref, proj_ref, norm_t_ref, slope_ref, query_ref, key_ref, query_t_ref):
+        masks = lane_masks()
+        for tile in range(tiles):
+            span = pl.ds(tile * TILE, TILE)
+            norm_t_ref[:, tile * TILE : (tile + 1) * TILE] = jnp.transpose(normed_ref[span, :])
+            slope_ref[span, :] = silu_grad(pre_ref[span, :])
+            query = proj_ref[span, 2 * part : 3 * part] * jnp.asarray(0.5 * scale, BF)
+            key = proj_ref[span, 3 * part :]
+            for head in range(heads):
+                query_ref[head, span, :] = jnp.where(masks[head], query, jnp.zeros_like(query))
+                query_t_ref[head, :, tile * TILE : (tile + 1) * TILE] = jnp.transpose(query_ref[head, span, :])
+                key_ref[head, span, :] = jnp.where(masks[head], key, jnp.zeros_like(key))
+
+    between_args = (normed_rows, pre, proj)
+    between_outs = [
+        shape((width, rows_all), BF),
+        shape((rows_all, 4 * part), F32),
+        shape((heads, rows_all, part), BF),
+        shape((heads, rows_all, part), BF),
+        shape((heads, part, rows_all), BF),
+    ]
+    norm_t, slope, *head_parts = call(
+        between_kernel, between_outs, between_args, 10 * rows_all * width, limit=room
+    )()(*between_args)
+
     grad_count = 4 if packed else 2
 
     def proj_places(chunk):
@@ -345,10 +372,11 @@
 
     def backward_kernel(*refs):
         stat_refs, cot_refs = refs[:ctx], refs[ctx : 2 * ctx]
-        begin_ref, att_ref, gg_ref, pre_ref, proj_ref, norm_t_ref = refs[2 * ctx : 2 * ctx + 6]
-        grad_refs, refs = refs[2 * ctx + 6 : 2 * ctx + 6 + grad_count], refs[2 * ctx + 6 + grad_count :]
+        begin_ref, att_ref, gg_ref, slope_ref, proj_ref, norm_t_ref = refs[2 * ctx : 2 * ctx + 6]
+        query_ref, key_ref, query_t_ref = refs[2 * ctx + 6 : 2 * ctx + 9]
+        grad_refs, refs = refs[2 * ctx + 9 : 2 * ctx + 9 + grad_count], refs[2 * ctx + 9 + grad_count :]
         row_refs = refs[:ctx]
-        query_ref, key_ref, grad_ref, dq_ref, gp_ref, gated_ref, late_ref, out_ref = refs[ctx:]
+        grad_ref, dq_ref, gp_ref, gated_ref, late_ref, out_ref = refs[ctx:]
         mine = lax.axis_index("ctx")
         masks = lane_masks()
 
@@ -374,11 +402,8 @@
             update = proj_ref[span, :part].astype(F32)
             gated_ref[span, :] = (normed * update).astype(BF)
             grad_att = ((grad * update - grad_c - normed * cross_c) * inverse_c).astype(BF)
-            gp_ref[span, :part] = (grad * normed * silu_grad(pre_ref[span, :part])).astype(BF)
-            query = proj_ref[span, 2 * part : 3 * part] * jnp.asarray(0.5 * scale, BF)
+            gp_ref[span, :part] = (grad * normed * slope_ref[span, :part]).astype(BF)
             for head in range(heads):
-                query_ref[head, span, :] = masked(query, head)
-                key_ref[head, span, :] = masked(proj_ref[span, 3 * part :], head)
                 grad_ref[head, span, :] = masked(grad_att, head)
             dq_ref[span, :] = jnp.zeros((half, part), F32)
         out_term = jnp.zeros((part, width), F32)
@@ -411,7 +436,7 @@
                     allowed = allowed & (key_pos <= query_pos)
                 grad_query = jnp.zeros((TILE, part), F32)
                 for head in range(heads):
-                    score = nt_dot(key, query_ref[head, span, :])
+                    score = nn_dot(key, query_t_ref[head, :, at * TILE : (at + 1) * TILE])
                     tanh = jnp.tanh(score)
                     cross = score * tanh
                     weight = jnp.where(allowed, score + cross, 0.0).astype(BF)
@@ -423,15 +448,15 @@
                     grad_query = grad_query + tn_dot(grad_score, key_ref[head, key_span, :])
                 dq_ref[span, :] = dq_ref[span, :] + grad_query
             gp_ref[key_span, part : 2 * part] = (
-                grad_value * silu_grad(pre_ref[key_span, part : 2 * part])
+                grad_value * slope_ref[key_span, part : 2 * part]
             ).astype(BF)
             gp_ref[key_span, 3 * part :] = (
-                grad_key * (2.0 / scale) * silu_grad(pre_ref[key_span, 3 * part :])
+                grad_key * (2.0 / scale) * slope_ref[key_span, 3 * part :]
             ).astype(BF)
         for tile in range(tiles):
             span = pl.ds(tile * TILE, TILE)
             gp_ref[span, 2 * part : 3 * part] = (
-                dq_ref[span, :] * silu_grad(pre_ref[span, 2 * part : 3 * part])
+                dq_ref[span, :] * slope_ref[span, 2 * part : 3 * part]
             ).astype(BF)
         for rel in range(ctx):
             for side in range(2):
@@ -455,7 +480,7 @@
                 for first, each in out_places(chunk):
                     to[first : first + out_step, :] = out_ref[out_rows, each * part : (each + 1) * part]
 
-    bwd_args = (*stats_of, *cot_of, begin_of, attended, grad_gated, pre, proj, norm_t)
+    bwd_args = (*stats_of, *cot_of, begin_of, attended, grad_gated, slope, proj, norm_t, *head_parts)
     if packed:
         bwd_outs = [shape((dps // 2, piece_rows, part), BF)] * 4
     else:
@@ -465,8 +490,6 @@
         backward_kernel, bwd_outs, bwd_args, 10 * rows_all * rows_all * part, limit=room
     )(
         scratch_shapes=[
-            pltpu.VMEM((heads, rows_all, part), BF),
-            pltpu.VMEM((heads, rows_all, part), BF),
             pltpu.VMEM((heads, rows_all, part), BF),
             pltpu.VMEM((rows_all, part), F32),
             pltpu.VMEM((rows_all, 4 * part), BF),

time: 122 us -> 126 us (1.033)
  waiting for transfers between devices: 50.4 us -> 52.5 us
  Pallas kernels: 23.6 us -> 24.9 us
    ppermute x39, waiting for transfers between devices: 50.4 us -> 52.5 us  [swap(): lax.ppermute(values, axis, [(each, each ^ distance) for each in range(siz...]
    pallas_call x0 -> x1, Pallas kernels: none -> 1.46 us  [local(): call(between_kernel, between_outs, between_args, 10 * rows_all * width, l...]
  transfers between devices with their start and end apart: 39 -> 39, of which waited for: 19 -> 21; matrix products, arithmetic and copies ran while one was open for 1% -> 1% of each run, Pallas kernels for 3% -> 4%
where the time goes in v1:
time: 126 us; the launch traced here: 125 us
  waiting for transfers between devices  52.5 us (42%)
  starting transfers between devices  43 us (34%)
  Pallas kernels  24.9 us (20%)
  local copies, waits for them, and re-layouts  4.14 us (3%)
    ppermute x39, waiting for transfers between devices, swap(): lax.ppermute(values, axis, [(each, each ^ distance) for each in range(siz...  52.5 us
    ppermute x39, starting transfers between devices, swap(): lax.ppermute(values, axis, [(each, each ^ distance) for each in range(siz...  43 us
    pallas_call x1, Pallas kernels, local(): call(backward_kernel, bwd_outs, bwd_args, 10 * rows_all * rows_all * part...  7.56 us
    pallas_call x1, Pallas kernels, local(): call(forward_kernel, fwd_outs, fwd_args, 4 * rows_all * rows_all * part,...  7.19 us
    unnamed x20, local copies, waits for them, and re-layouts  4.13 us
    pallas_call x1, Pallas kernels, local(): call(finish_kernel, [shape((width, 4 * width), F32), shape((width, width)...  3.08 us
  transfers between devices with their start and end apart: 39, of which 21 were waited for; matrix products, arithmetic and copies ran while one was open for 1% of the time, Pallas kernels for 4%

profile of v1, /device:TPU:0, one launch (start us, length us, event | category | flops | bytes accessed | tf_op | source)
XLA Modules:
  0.0 125.5 jit_solution(2330227165296984294)
XLA Ops:
  0.6 2.3 %shard_map.102 = (bf16[48,512]{1,0:T(8,128)(2,1)}, bf16[48,512]{1,0:T(8,128)(2,1)}, bf16[48,512]{1,0:T(8,128)(2,1)}, bf16[48,512]{1,0:T(8,128)(2,1)}, bf16[48,51...) custom-call(s32[1,256]{1,0:T(1,128)} %bitcast.2, ...), custom_call_target="tpu_custom_call" | custom-call | flops 100663296 | bytes 1198080 | tf_op jit(solution)/shard_map/pallas_call | solution.py:187
  2.9 4.1 %collective-permute-start.6 = (bf16[48,512]{1,0:T(8,128)(2,1)}, bf16[48,512]{1,0:T(8,128)(2,1)S(1)}, u32[]{:S(2)}, u32[]{:S(2)}) collective-permute-start(bf16[48,512]{1,0:T(8,128)(2,1)} %get-tuple-element.48), channel_id=1, source_target_pairs={{0,16},{4,20},{8,24},{12,28},{16,0},{20,4},{24,8},{28,12},{1,17},{... | collective-permute-start | bytes 147464 | tf_op jit(solution)/shard_map/ppermute | solution.py:35
  7.1 3.1 %collective-permute-start.8 = (bf16[48,512]{1,0:T(8,128)(2,1)}, bf16[48,512]{1,0:T(8,128)(2,1)S(1)}, u32[]{:S(2)}, u32[]{:S(2)}) collective-permute-start(bf16[48,512]{1,0:T(8,128)(2,1)} %get-tuple-element.50), channel_id=1, source_target_pairs={{0,24},{4,28},{8,16},{12,20},{16,8},{20,12},{24,0},{28,4},{1,25},{... | collective-permute-start | bytes 147464 | tf_op jit(solution)/shard_map/ppermute | solution.py:35
  11.0 0.8 constant_dynamic-update-slice_fusion.3
  12.1 2.1 %collective-permute-done.7 = bf16[48,512]{1,0:T(8,128)(2,1)S(1)} collective-permute-done((bf16[48,512]{1,0:T(8,128)(2,1)}, bf16[48,512]{1,0:T(8,128)(2,1)S(1)}, u32[]{:S(2)}, u32[]{:S(2)}) %collective-permute-start.7) | collective-permute-done | bytes 49184 | tf_op jit(solution)/shard_map/ppermute | solution.py:35
  14.2 1.6 %collective-permute-done.9 = bf16[48,512]{1,0:T(8,128)(2,1)S(1)} collective-permute-done((bf16[48,512]{1,0:T(8,128)(2,1)}, bf16[48,512]{1,0:T(8,128)(2,1)S(1)}, u32[]{:S(2)}, u32[]{:S(2)}) %collective-permute-start.9) | collective-permute-done | bytes 49184 | tf_op jit(solution)/shard_map/ppermute | solution.py:35
  15.8 1.5 %collective-permute-start.11 = (bf16[192,512]{1,0:T(8,128)(2,1)S(1)}, bf16[192,512]{1,0:T(8,128)(2,1)S(1)}, u32[]{:S(2)}, u32[]{:S(2)}) collective-permute-start(bf16[192,512]{1,0:T(8,128)(2,1)S(1)} %constant_dynamic-update-slice_fusion.4.refs_4_), channel_id=1, source_target_pairs={{0,2},{1,3},{2,0},{3,1},{4,6},{5,7},{6,4},{7,5},{8,10},{9,11},{10,... | collective-permute-start | bytes 589832 | tf_op jit(solution)/shard_map/ppermute | solution.py:35
  18.0 1.5 %collective-permute-start.3 = (bf16[192,512]{1,0:T(8,128)(2,1)S(1)}, bf16[192,512]{1,0:T(8,128)(2,1)S(1)}, u32[]{:S(2)}, u32[]{:S(2)}) collective-permute-start(bf16[192,512]{1,0:T(8,128)(2,1)S(1)} %constant_dynamic-update-slice_fusion.refs_0_), channel_id=1, source_target_pairs={{0,1},{1,0},{2,3},{3,2},{4,5},{5,4},{6,7},{7,6},{8,9},{9,8},{10,11... | collective-permute-start | bytes 589832 | tf_op jit(solution)/shard_map/ppermute | solution.py:35
  20.1 1.5 %collective-permute-start.4 = (bf16[192,512]{1,0:T(8,128)(2,1)S(1)}, bf16[192,512]{1,0:T(8,128)(2,1)S(1)}, u32[]{:S(2)}, u32[]{:S(2)}) collective-permute-start(bf16[192,512]{1,0:T(8,128)(2,1)S(1)} %constant_dynamic-update-slice_fusion.refs_0_), channel_id=1, source_target_pairs={{0,2},{1,3},{2,0},{3,1},{4,6},{5,7},{6,4},{7,5},{8,10},{9,11},{10,... | collective-permute-start | bytes 589832 | tf_op jit(solution)/shard_map/ppermute | solution.py:35
  21.6 1.5 %collective-permute-start.13 = (bf16[272,512]{1,0:T(8,128)(2,1)}, bf16[272,512]{1,0:T(8,128)(2,1)S(1)}, u32[]{:S(2)}, u32[]{:S(2)}) collective-permute-start(bf16[272,512]{1,0:T(8,128)(2,1)} %get-tuple-element.52.refs_8_.refs_4_), channel_id=1, source_target_pairs={{0,1},{1,0},{2,3},{3,2},{4,5},{5,4},{6,7},{7,6},{8,9},{9,8},{10,11... | collective-permute-start | bytes 835592 | tf_op jit(solution)/shard_map/ppermute | solution.py:35
  23.6 1.5 %collective-permute-start.14 = (bf16[272,512]{1,0:T(8,128)(2,1)}, bf16[272,512]{1,0:T(8,128)(2,1)S(1)}, u32[]{:S(2)}, u32[]{:S(2)}) collective-permute-start(bf16[272,512]{1,0:T(8,128)(2,1)} %get-tuple-element.52.refs_8_.refs_4_), channel_id=1, source_target_pairs={{0,2},{1,3},{2,0},{3,1},{4,6},{5,7},{6,4},{7,5},{8,10},{9,11},{10,... | collective-permute-start | bytes 835592 | tf_op jit(solution)/shard_map/ppermute | solution.py:35
  25.8 2.4 %collective-permute-start.15 = (bf16[272,512]{1,0:T(8,128)(2,1)}, bf16[272,512]{1,0:T(8,128)(2,1)S(1)}, u32[]{:S(2)}, u32[]{:S(2)}) collective-permute-start(bf16[272,512]{1,0:T(8,128)(2,1)} %get-tuple-element.52.refs_8_.refs_4_), channel_id=1, source_target_pairs={{0,3},{1,2},{2,1},{3,0},{4,7},{5,6},{6,5},{7,4},{8,11},{9,10},{10,... | collective-permute-start | bytes 835592 | tf_op jit(solution)/shard_map/ppermute | solution.py:35
  28.2 1.8 %collective-permute-done.10.refs_5_ = bf16[192,512]{1,0:T(8,128)(2,1)S(1)} collective-permute-done((bf16[192,512]{1,0:T(8,128)(2,1)S(1)}, bf16[192,512]{1,0:T(8,128)(2,1)S(1)}, u32[]{:S(2)}, u32[]{:S(2)}) %collective-permute-start.10) | collective-permute-done | bytes 196640 | tf_op jit(solution)/shard_map/ppermute | solution.py:35
  30.0 1.5 %collective-permute-start.12 = (bf16[192,512]{1,0:T(8,128)(2,1)S(1)}, bf16[192,512]{1,0:T(8,128)(2,1)S(1)}, u32[]{:S(2)}, u32[]{:S(2)}) collective-permute-start(bf16[192,512]{1,0:T(8,128)(2,1)S(1)} %collective-permute-done.11.refs_6_), channel_id=1, source_target_pairs={{0,1},{1,0},{2,3},{3,2},{4,5},{5,4},{6,7},{7,6},{8,9},{9,8},{10,11... | collective-permute-start | bytes 589832 | tf_op jit(solution)/shard_map/ppermute | solution.py:35
  31.5 1.5 %collective-permute-start.5 = (bf16[192,512]{1,0:T(8,128)(2,1)S(1)}, bf16[192,512]{1,0:T(8,128)(2,1)S(1)}, u32[]{:S(2)}, u32[]{:S(2)}) collective-permute-start(bf16[192,512]{1,0:T(8,128)(2,1)S(1)} %collective-permute-done.3.refs_1_), channel_id=1, source_target_pairs={{0,2},{1,3},{2,0},{3,1},{4,6},{5,7},{6,4},{7,5},{8,10},{9,11},{10,... | collective-permute-start | bytes 589832 | tf_op jit(solution)/shard_map/ppermute | solution.py:35
  33.0 1.6 %copy-done = bf16[512,2048]{1,0:T(8,128)(2,1)S(1)} copy-done((bf16[512,2048]{1,0:T(8,128)(2,1)S(1)}, bf16[512,2048]{1,0:T(8,128)(2,1)}, u32[]{:S(2)}) %copy-start) | copy-done | bytes 2097176
  34.6 1.0 copy-done.2
  36.3 0.7 shard_map.103
  37.0 5.9 %collective-permute-done.15.refs_11_.refs_7_ = bf16[272,512]{1,0:T(8,128)(2,1)S(1)} collective-permute-done((bf16[272,512]{1,0:T(8,128)(2,1)}, bf16[272,512]{1,0:T(8,128)(2,1)S(1)}, u32[]{:S(2)}, u32[]{:S(2)}) %collective-permute-start.15) | collective-permute-done | bytes 278560 | tf_op jit(solution)/shard_map/ppermute | solution.py:35
  43.0 2.0 %collective-permute-done.12.refs_7_ = bf16[192,512]{1,0:T(8,128)(2,1)S(1)} collective-permute-done((bf16[192,512]{1,0:T(8,128)(2,1)S(1)}, bf16[192,512]{1,0:T(8,128)(2,1)S(1)}, u32[]{:S(2)}, u32[]{:S(2)}) %collective-permute-start.12) | collective-permute-done | bytes 196640 | tf_op jit(solution)/shard_map/ppermute | solution.py:35
  45.0 7.2 %shard_map.104 = (bf16[256,512]{1,0:T(8,128)(2,1)S(1)}, bf16[1024,512]{1,0:T(8,128)(2,1)S(1)}, f32[1024,512]{1,0:T(8,128)S(1)}, bf16[1024,512]{1,0:T(8,128)(2,1)...) custom-call(bf16[192,512]{1,0:T(8,128)(2,1)S(1)} %constant_dynamic-update-slice_fusion.refs_0_, ...), custom_call_target="tpu_custom_call" | custom-call | flops 536870912 | bytes 8867840 | tf_op jit(solution)/shard_map/pallas_call | solution.py:326
  52.2 1.5 %collective-permute-start.16 = (f32[4,8,128]{2,1,0:T(8,128)S(1)}, f32[4,8,128]{2,1,0:T(8,128)S(1)}, u32[]{:S(2)}, u32[]{:S(2)}) collective-permute-start(f32[4,8,128]{2,1,0:T(8,128)S(1)} %get-tuple-element.56.refs_0_), channel_id=1, source_target_pairs={{0,1},{1,0},{2,3},{3,2},{4,5},{5,4},{6,7},{7,6},{8,9},{9,8},{10,11... | collective-permute-start | bytes 49160 | tf_op jit(solution)/shard_map/ppermute | solution.py:35
  53.7 1.5 %collective-permute-start.17 = (f32[4,8,128]{2,1,0:T(8,128)S(1)}, f32[4,8,128]{2,1,0:T(8,128)S(1)}, u32[]{:S(2)}, u32[]{:S(2)}) collective-permute-start(f32[4,8,128]{2,1,0:T(8,128)S(1)} %get-tuple-element.56.refs_0_), channel_id=1, source_target_pairs={{0,2},{1,3},{2,0},{3,1},{4,6},{5,7},{6,4},{7,5},{8,10},{9,11},{10,... | collective-permute-start | bytes 49160 | tf_op jit(solution)/shard_map/ppermute | solution.py:35
  55.7 1.5 %shard_map.105 = (bf16[512,1024]{1,0:T(8,128)(2,1)S(1)}, f32[1024,512]{1,0:T(8,128)S(1)}, bf16[2,1024,128]{2,1,0:T(8,128)(2,1)S(1)}, bf16[2,1024,128]{2,1,0:T(8,128)(2,1)S(1)}, bf16[2,128,1024]{2,1,0:T(8,128)(2,1)S(1)}) custom-call(bf16[1024,512]{1,0:T(8,128)(2,1)S(1)} %get-tuple-element.59.normed_ref, f32[1024,512]{1,0:T(8,128)S(1)} %get-tuple-element.60.pre_ref, ...), custom_call_target="tpu_custom_call" | custom-call | flops 5242880 | bytes 8912896 | tf_op jit(solution)/shard_map/pallas_call | solution.py:361
  57.4 2.4 %collective-permute-done.18.refs_3_ = f32[4,8,128]{2,1,0:T(8,128)S(1)} collective-permute-done((f32[4,8,128]{2,1,0:T(8,128)S(1)}, f32[4,8,128]{2,1,0:T(8,128)S(1)}, u32[]{:S(2)}, u32[]{:S(2)}) %collective-permute-start.18) | collective-permute-done | bytes 16416 | tf_op jit(solution)/shard_map/ppermute | solution.py:35
  59.8 7.6 %shard_map.106 = (bf16[4,160,128]{2,1,0:T(8,128)(2,1)S(1)}, bf16[4,160,128]{2,1,0:T(8,128)(2,1)S(1)}, bf16[4,160,128]{2,1,0:T(8,128)(2,1)S(1)}, bf16[4,160,128]{...) custom-call(f32[4,8,128]{2,1,0:T(8,128)S(1)} %get-tuple-element.56.r, ...), custom_call_target="tpu_custom_call" | custom-call | flops 1342177280 | bytes 9965568 | tf_op jit(solution)/shard_map/pallas_call | solution.py:489
  68.0 0.9 collective-permute-done.29.got_ref
  69.6 1.5 %collective-permute-start.23 = (bf16[2,160,128]{2,1,0:T(8,128)(2,1)S(1)}, bf16[2,160,128]{2,1,0:T(8,128)(2,1)S(1)}, u32[]{:S(2)}, u32[]{:S(2)}) collective-permute-start(bf16[2,160,128]{2,1,0:T(8,128)(2,1)S(1)} %get-tuple-element.77), channel_id=1, source_target_pairs={{0,8},{4,12},{8,0},{12,4},{16,24},{20,28},{24,16},{28,20},{1,9},{5... | collective-permute-start | bytes 245768 | tf_op jit(solution)/shard_map/ppermute | solution.py:35
  71.1 3.2 %collective-permute-done.30.got_ref = bf16[2,160,128]{2,1,0:T(8,128)(2,1)S(1)} collective-permute-done((bf16[2,160,128]{2,1,0:T(8,128)(2,1)S(1)}, bf16[2,160,128]{2,1,0:T(8,128)(2,1)S(1)}, u32[]{:S(2)}, u32[]{:S(2)}) %collective-permute-start.30) | collective-permute-done | bytes 81952 | tf_op jit(solution)/shard_map/ppermute | solution.py:35
  74.3 2.5 %collective-permute-start.31 = (bf16[2,160,128]{2,1,0:T(8,128)(2,1)S(1)}, bf16[2,160,128]{2,1,0:T(8,128)(2,1)S(1)}, u32[]{:S(2)}, u32[]{:S(2)}) collective-permute-start(bf16[2,160,128]{2,1,0:T(8,128)(2,1)S(1)} %shard_map.112.keep_ref), channel_id=1, source_target_pairs={{0,16},{4,20},{8,24},{12,28},{16,0},{20,4},{24,8},{28,12},{1,17},{... | collective-permute-start | bytes 245768 | tf_op jit(solution)/shard_map/ppermute | solution.py:35
  76.9 1.7 %collective-permute-start.24 = (bf16[2,160,128]{2,1,0:T(8,128)(2,1)S(1)}, bf16[2,160,128]{2,1,0:T(8,128)(2,1)S(1)}, u32[]{:S(2)}, u32[]{:S(2)}) collective-permute-start(bf16[2,160,128]{2,1,0:T(8,128)(2,1)S(1)} %shard_map.109.keep_ref), channel_id=1, source_target_pairs={{0,16},{4,20},{8,24},{12,28},{16,0},{20,4},{24,8},{28,12},{1,17},{... | collective-permute-start | bytes 245768 | tf_op jit(solution)/shard_map/ppermute | solution.py:35
  78.5 4.3 %collective-permute-done.31.got_ref = bf16[2,160,128]{2,1,0:T(8,128)(2,1)S(1)} collective-permute-done((bf16[2,160,128]{2,1,0:T(8,128)(2,1)S(1)}, bf16[2,160,128]{2,1,0:T(8,128)(2,1)S(1)}, u32[]{:S(2)}, u32[]{:S(2)}) %collective-permute-start.31) | collective-permute-done | bytes 81952 | tf_op jit(solution)/shard_map/ppermute | solution.py:35
  82.9 0.8 collective-permute-done.24.got_ref
  83.7 1.3 %collective-permute-start.25 = (bf16[2,160,128]{2,1,0:T(8,128)(2,1)S(1)}, bf16[2,160,128]{2,1,0:T(8,128)(2,1)S(1)}, u32[]{:S(2)}, u32[]{:S(2)}) collective-permute-start(bf16[2,160,128]{2,1,0:T(8,128)(2,1)S(1)} %shard_map.110), channel_id=1, source_target_pairs={{0,8},{4,12},{8,0},{12,4},{16,24},{20,28},{24,16},{28,20},{1,9},{5... | collective-permute-start | bytes 245768 | tf_op jit(solution)/shard_map/ppermute | solution.py:35
  85.0 2.3 %collective-permute-done.32 = bf16[2,160,128]{2,1,0:T(8,128)(2,1)S(1)} collective-permute-done((bf16[2,160,128]{2,1,0:T(8,128)(2,1)S(1)}, bf16[2,160,128]{2,1,0:T(8,128)(2,1)S(1)}, u32[]{:S(2)}, u32[]{:S(2)}) %collective-permute-start.32) | collective-permute-done | bytes 81952 | tf_op jit(solution)/shard_map/ppermute | solution.py:35
  87.4 0.8 collective-permute-start.33
  88.9 1.5 %collective-permute-start.34 = (bf16[4,160,128]{2,1,0:T(8,128)(2,1)S(1)}, bf16[4,160,128]{2,1,0:T(8,128)(2,1)S(1)}, u32[]{:S(2)}, u32[]{:S(2)}) collective-permute-start(bf16[4,160,128]{2,1,0:T(8,128)(2,1)S(1)} %pad_maximum_fusion.4.refs_4_), channel_id=1, source_target_pairs={{0,1},{1,0},{2,3},{3,2},{4,5},{5,4},{6,7},{7,6},{8,9},{9,8},{10,11... | collective-permute-start | bytes 491528 | tf_op jit(solution)/shard_map/ppermute | solution.py:35
  90.3 1.2 collective-permute-start.27
  92.1 1.8 %collective-permute-done.33.refs_5_ = bf16[4,160,128]{2,1,0:T(8,128)(2,1)S(1)} collective-permute-done((bf16[4,160,128]{2,1,0:T(8,128)(2,1)S(1)}, bf16[4,160,128]{2,1,0:T(8,128)(2,1)S(1)}, u32[]{:S(2)}, u32[]{:S(2)}) %collective-permute-start.33) | collective-permute-done | bytes 163872 | tf_op jit(solution)/shard_map/ppermute | solution.py:35
  93.9 1.5 %collective-permute-done.26.refs_1_ = bf16[4,160,128]{2,1,0:T(8,128)(2,1)S(1)} collective-permute-done((bf16[4,160,128]{2,1,0:T(8,128)(2,1)S(1)}, bf16[4,160,128]{2,1,0:T(8,128)(2,1)S(1)}, u32[]{:S(2)}, u32[]{:S(2)}) %collective-permute-start.26) | collective-permute-done | bytes 163872 | tf_op jit(solution)/shard_map/ppermute | solution.py:35
  95.4 3.5 %collective-permute-done.34.refs_6_ = bf16[4,160,128]{2,1,0:T(8,128)(2,1)S(1)} collective-permute-done((bf16[4,160,128]{2,1,0:T(8,128)(2,1)S(1)}, bf16[4,160,128]{2,1,0:T(8,128)(2,1)S(1)}, u32[]{:S(2)}, u32[]{:S(2)}) %collective-permute-start.34) | collective-permute-done | bytes 163872 | tf_op jit(solution)/shard_map/ppermute | solution.py:35
  99.7 1.2 collective-permute-start.28
  100.9 0.8 collective-permute-start.20
  101.7 4.7 %collective-permute-done.35.refs_7_ = bf16[4,160,128]{2,1,0:T(8,128)(2,1)S(1)} collective-permute-done((bf16[4,160,128]{2,1,0:T(8,128)(2,1)S(1)}, bf16[4,160,128]{2,1,0:T(8,128)(2,1)S(1)}, u32[]{:S(2)}, u32[]{:S(2)}) %collective-permute-start.35) | collective-permute-done | bytes 163872 | tf_op jit(solution)/shard_map/ppermute | solution.py:35
  106.5 1.4 %collective-permute-start.21 = (bf16[256,640]{1,0:T(8,128)(2,1)S(1)}, bf16[256,640]{1,0:T(8,128)(2,1)S(1)}, u32[]{:S(2)}, u32[]{:S(2)}) collective-permute-start(bf16[256,640]{1,0:T(8,128)(2,1)S(1)} %get-tuple-element.70), channel_id=1, source_target_pairs={{0,3},{1,2},{2,1},{3,0},{4,7},{5,6},{6,5},{7,4},{8,11},{9,10},{10,... | collective-permute-start | bytes 983048 | tf_op jit(solution)/shard_map/ppermute | solution.py:35
  108.5 11.5 %collective-permute-done.20.refs_2_ = bf16[256,640]{1,0:T(8,128)(2,1)S(1)} collective-permute-done((bf16[256,640]{1,0:T(8,128)(2,1)S(1)}, bf16[256,640]{1,0:T(8,128)(2,1)S(1)}, u32[]{:S(2)}, u32[]{:S(2)}) %collective-permute-start.20) | collective-permute-done | bytes 327712 | tf_op jit(solution)/shard_map/ppermute | solution.py:35
  120.0 2.4 %shard_map.107 = (bf16[256,512]{1,0:T(8,128)(2,1)}, bf16[256,512]{1,0:T(8,128)(2,1)}) custom-call(bf16[256,640]{1,0:T(8,128)(2,1)S(1)} %get-tuple-element.67.refs_0_, bf16[256,640]{1,0:T(8,128)(2,1)S(1)} %collective-permute-done.19.refs_1_, bf16[256,640]{1,0:T(8,128)(2,1)S(1)} %collective-permute-done.20.refs_2_, ...), custom_call_target="tpu_custom_call" | custom-call | flops 671088640 | bytes 4980736 | tf_op jit(solution)/shard_map/pallas_call | solution.py:567
  122.4 3.1 %shard_map.114 = (f32[512,2048]{1,0:T(8,128)}, f32[512,512]{1,0:T(8,128)}) custom-call(bf16[4,160,128]{2,1,0:T(8,128)(2,1)S(1)} %pad_maximum_fusion.3.refs_0_, bf16[4,160,128]{2,1,0:T(8,128)(2,1)S(1)} %collective-permute-done.26.refs_1_, bf16[4,160,128]{2,1,0:T(8,128)(2,1)S(1)} %collective-permute-done.27.refs_2_, ...), custom_call_target="tpu_custom_call" | custom-call | flops 2621440 | bytes 7864320 | tf_op jit(solution)/shard_map/pallas_call | solution.py:605
  (70 shorter events, 9.1 us)
Async XLA Ops:
  2.9 42.0 %copy-start.4 = (bf16[272,512]{1,0:T(8,128)(2,1)S(1)}, bf16[272,512]{1,0:T(8,128)(2,1)}, u32[]{:S(2)}) copy-start(bf16[272,512]{1,0:T(8,128)(2,1)} %get-tuple-element.52.refs_8_.refs_4_) | copy-start | bytes 835588
  2.9 8.9 %collective-permute-start.6 = (bf16[48,512]{1,0:T(8,128)(2,1)}, bf16[48,512]{1,0:T(8,128)(2,1)S(1)}, u32[]{:S(2)}, u32[]{:S(2)}) collective-permute-start(bf16[48,512]{1,0:T(8,128)(2,1)} %get-tuple-element.48), channel_id=1, source_target_pairs={{0,16},{4,20},{8,24},{12,28},{16,0},{20,4},{24,8},{28,12},{1,17},{... | collective-permute-start | bytes 147464 | tf_op jit(solution)/shard_map/ppermute | solution.py:35
  7.1 7.1 %collective-permute-start.7 = (bf16[48,512]{1,0:T(8,128)(2,1)}, bf16[48,512]{1,0:T(8,128)(2,1)S(1)}, u32[]{:S(2)}, u32[]{:S(2)}) collective-permute-start(bf16[48,512]{1,0:T(8,128)(2,1)} %get-tuple-element.49), channel_id=1, source_target_pairs={{0,20},{4,16},{8,28},{12,24},{16,4},{20,0},{24,12},{28,8},{1,21},{... | collective-permute-start | bytes 147464 | tf_op jit(solution)/shard_map/ppermute | solution.py:35
  7.1 7.1 %collective-permute-start.8 = (bf16[48,512]{1,0:T(8,128)(2,1)}, bf16[48,512]{1,0:T(8,128)(2,1)S(1)}, u32[]{:S(2)}, u32[]{:S(2)}) collective-permute-start(bf16[48,512]{1,0:T(8,128)(2,1)} %get-tuple-element.50), channel_id=1, source_target_pairs={{0,24},{4,28},{8,16},{12,20},{16,8},{20,12},{24,0},{28,4},{1,25},{... | collective-permute-start | bytes 147464 | tf_op jit(solution)/shard_map/ppermute | solution.py:35
  10.2 5.6 %collective-permute-start.9 = (bf16[48,512]{1,0:T(8,128)(2,1)}, bf16[48,512]{1,0:T(8,128)(2,1)S(1)}, u32[]{:S(2)}, u32[]{:S(2)}) collective-permute-start(bf16[48,512]{1,0:T(8,128)(2,1)} %get-tuple-element.51), channel_id=1, source_target_pairs={{0,28},{4,24},{8,20},{12,16},{16,12},{20,8},{24,4},{28,0},{1,29},{... | collective-permute-start | bytes 147464 | tf_op jit(solution)/shard_map/ppermute | solution.py:35
  10.7 6.6 %collective-permute-start = (bf16[48,512]{1,0:T(8,128)(2,1)}, bf16[48,512]{1,0:T(8,128)(2,1)S(1)}, u32[]{:S(2)}, u32[]{:S(2)}) collective-permute-start(bf16[48,512]{1,0:T(8,128)(2,1)} %get-tuple-element.45), channel_id=1, source_target_pairs={{0,4},{4,0},{8,12},{12,8},{16,20},{20,16},{24,28},{28,24},{1,5},{5... | collective-permute-start | bytes 147464 | tf_op jit(solution)/shard_map/ppermute | solution.py:35
  11.8 5.5 %collective-permute-start.1 = (bf16[48,512]{1,0:T(8,128)(2,1)}, bf16[48,512]{1,0:T(8,128)(2,1)S(1)}, u32[]{:S(2)}, u32[]{:S(2)}) collective-permute-start(bf16[48,512]{1,0:T(8,128)(2,1)} %get-tuple-element.46), channel_id=1, source_target_pairs={{0,8},{4,12},{8,0},{12,4},{16,24},{20,28},{24,16},{28,20},{1,9},{5... | collective-permute-start | bytes 147464 | tf_op jit(solution)/shard_map/ppermute | solution.py:35
  14.2 3.9 %collective-permute-start.2 = (bf16[48,512]{1,0:T(8,128)(2,1)}, bf16[48,512]{1,0:T(8,128)(2,1)S(1)}, u32[]{:S(2)}, u32[]{:S(2)}) collective-permute-start(bf16[48,512]{1,0:T(8,128)(2,1)} %get-tuple-element.47), channel_id=1, source_target_pairs={{0,12},{4,8},{8,4},{12,0},{16,28},{20,24},{24,20},{28,16},{1,13},{... | collective-permute-start | bytes 147464 | tf_op jit(solution)/shard_map/ppermute | solution.py:35
  15.8 7.8 %collective-permute-start.11 = (bf16[192,512]{1,0:T(8,128)(2,1)S(1)}, bf16[192,512]{1,0:T(8,128)(2,1)S(1)}, u32[]{:S(2)}, u32[]{:S(2)}) collective-permute-start(bf16[192,512]{1,0:T(8,128)(2,1)S(1)} %constant_dynamic-update-slice_fusion.4.refs_4_), channel_id=1, source_target_pairs={{0,2},{1,3},{2,0},{3,1},{4,6},{5,7},{6,4},{7,5},{8,10},{9,11},{10,... | collective-permute-start | bytes 589832 | tf_op jit(solution)/shard_map/ppermute | solution.py:35
  18.0 7.8 %collective-permute-start.3 = (bf16[192,512]{1,0:T(8,128)(2,1)S(1)}, bf16[192,512]{1,0:T(8,128)(2,1)S(1)}, u32[]{:S(2)}, u32[]{:S(2)}) collective-permute-start(bf16[192,512]{1,0:T(8,128)(2,1)S(1)} %constant_dynamic-update-slice_fusion.refs_0_), channel_id=1, source_target_pairs={{0,1},{1,0},{2,3},{3,2},{4,5},{5,4},{6,7},{7,6},{8,9},{9,8},{10,11... | collective-permute-start | bytes 589832 | tf_op jit(solution)/shard_map/ppermute | solution.py:35
  19.5 10.5 %collective-permute-start.10 = (bf16[192,512]{1,0:T(8,128)(2,1)S(1)}, bf16[192,512]{1,0:T(8,128)(2,1)S(1)}, u32[]{:S(2)}, u32[]{:S(2)}) collective-permute-start(bf16[192,512]{1,0:T(8,128)(2,1)S(1)} %constant_dynamic-update-slice_fusion.4.refs_4_), channel_id=1, source_target_pairs={{0,1},{1,0},{2,3},{3,2},{4,5},{5,4},{6,7},{7,6},{8,9},{9,8},{10,11... | collective-permute-start | bytes 589832 | tf_op jit(solution)/shard_map/ppermute | solution.py:35
  20.1 11.5 %collective-permute-start.4 = (bf16[192,512]{1,0:T(8,128)(2,1)S(1)}, bf16[192,512]{1,0:T(8,128)(2,1)S(1)}, u32[]{:S(2)}, u32[]{:S(2)}) collective-permute-start(bf16[192,512]{1,0:T(8,128)(2,1)S(1)} %constant_dynamic-update-slice_fusion.refs_0_), channel_id=1, source_target_pairs={{0,2},{1,3},{2,0},{3,1},{4,6},{5,7},{6,4},{7,5},{8,10},{9,11},{10,... | collective-permute-start | bytes 589832 | tf_op jit(solution)/shard_map/ppermute | solution.py:35
  21.6 15.4 %collective-permute-start.13 = (bf16[272,512]{1,0:T(8,128)(2,1)}, bf16[272,512]{1,0:T(8,128)(2,1)S(1)}, u32[]{:S(2)}, u32[]{:S(2)}) collective-permute-start(bf16[272,512]{1,0:T(8,128)(2,1)} %get-tuple-element.52.refs_8_.refs_4_), channel_id=1, source_target_pairs={{0,1},{1,0},{2,3},{3,2},{4,5},{5,4},{6,7},{7,6},{8,9},{9,8},{10,11... | collective-permute-start | bytes 835592 | tf_op jit(solution)/shard_map/ppermute | solution.py:35
  23.6 13.4 %collective-permute-start.14 = (bf16[272,512]{1,0:T(8,128)(2,1)}, bf16[272,512]{1,0:T(8,128)(2,1)S(1)}, u32[]{:S(2)}, u32[]{:S(2)}) collective-permute-start(bf16[272,512]{1,0:T(8,128)(2,1)} %get-tuple-element.52.refs_8_.refs_4_), channel_id=1, source_target_pairs={{0,2},{1,3},{2,0},{3,1},{4,6},{5,7},{6,4},{7,5},{8,10},{9,11},{10,... | collective-permute-start | bytes 835592 | tf_op jit(solution)/shard_map/ppermute | solution.py:35
  25.8 17.1 %collective-permute-start.15 = (bf16[272,512]{1,0:T(8,128)(2,1)}, bf16[272,512]{1,0:T(8,128)(2,1)S(1)}, u32[]{:S(2)}, u32[]{:S(2)}) collective-permute-start(bf16[272,512]{1,0:T(8,128)(2,1)} %get-tuple-element.52.refs_8_.refs_4_), channel_id=1, source_target_pairs={{0,3},{1,2},{2,1},{3,0},{4,7},{5,6},{6,5},{7,4},{8,11},{9,10},{10,... | collective-permute-start | bytes 835592 | tf_op jit(solution)/shard_map/ppermute | solution.py:35
  30.0 14.9 %collective-permute-start.12 = (bf16[192,512]{1,0:T(8,128)(2,1)S(1)}, bf16[192,512]{1,0:T(8,128)(2,1)S(1)}, u32[]{:S(2)}, u32[]{:S(2)}) collective-permute-start(bf16[192,512]{1,0:T(8,128)(2,1)S(1)} %collective-permute-done.11.refs_6_), channel_id=1, source_target_pairs={{0,1},{1,0},{2,3},{3,2},{4,5},{5,4},{6,7},{7,6},{8,9},{9,8},{10,11... | collective-permute-start | bytes 589832 | tf_op jit(solution)/shard_map/ppermute | solution.py:35
  31.5 13.5 %collective-permute-start.5 = (bf16[192,512]{1,0:T(8,128)(2,1)S(1)}, bf16[192,512]{1,0:T(8,128)(2,1)S(1)}, u32[]{:S(2)}, u32[]{:S(2)}) collective-permute-start(bf16[192,512]{1,0:T(8,128)(2,1)S(1)} %collective-permute-done.3.refs_1_), channel_id=1, source_target_pairs={{0,2},{1,3},{2,0},{3,1},{4,6},{5,7},{6,4},{7,5},{8,10},{9,11},{10,... | collective-permute-start | bytes 589832 | tf_op jit(solution)/shard_map/ppermute | solution.py:35
  33.0 1.6 %copy-start = (bf16[512,2048]{1,0:T(8,128)(2,1)S(1)}, bf16[512,2048]{1,0:T(8,128)(2,1)}, u32[]{:S(2)}) copy-start(bf16[512,2048]{1,0:T(8,128)(2,1)} %refs_6_.1) | copy-start | bytes 6291460
  34.6 1.0 copy-start.2
  35.7 0.7 copy-start.6
  52.2 5.0 %collective-permute-start.16 = (f32[4,8,128]{2,1,0:T(8,128)S(1)}, f32[4,8,128]{2,1,0:T(8,128)S(1)}, u32[]{:S(2)}, u32[]{:S(2)}) collective-permute-start(f32[4,8,128]{2,1,0:T(8,128)S(1)} %get-tuple-element.56.refs_0_), channel_id=1, source_target_pairs={{0,1},{1,0},{2,3},{3,2},{4,5},{5,4},{6,7},{7,6},{8,9},{9,8},{10,11... | collective-permute-start | bytes 49160 | tf_op jit(solution)/shard_map/ppermute | solution.py:35
  53.7 3.7 %collective-permute-start.17 = (f32[4,8,128]{2,1,0:T(8,128)S(1)}, f32[4,8,128]{2,1,0:T(8,128)S(1)}, u32[]{:S(2)}, u32[]{:S(2)}) collective-permute-start(f32[4,8,128]{2,1,0:T(8,128)S(1)} %get-tuple-element.56.refs_0_), channel_id=1, source_target_pairs={{0,2},{1,3},{2,0},{3,1},{4,6},{5,7},{6,4},{7,5},{8,10},{9,11},{10,... | collective-permute-start | bytes 49160 | tf_op jit(solution)/shard_map/ppermute | solution.py:35
  55.2 4.6 %collective-permute-start.18 = (f32[4,8,128]{2,1,0:T(8,128)S(1)}, f32[4,8,128]{2,1,0:T(8,128)S(1)}, u32[]{:S(2)}, u32[]{:S(2)}) collective-permute-start(f32[4,8,128]{2,1,0:T(8,128)S(1)} %get-tuple-element.56.refs_0_), channel_id=1, source_target_pairs={{0,3},{1,2},{2,1},{3,0},{4,7},{5,6},{6,5},{7,4},{8,11},{9,10},{10,... | collective-permute-start | bytes 49160 | tf_op jit(solution)/shard_map/ppermute | solution.py:35
  67.4 1.5 %collective-permute-start.29 = (bf16[4,160,128]{2,1,0:T(8,128)(2,1)S(1)}, bf16[4,160,128]{2,1,0:T(8,128)(2,1)S(1)}, u32[]{:S(2)}, u32[]{:S(2)}) collective-permute-start(bf16[4,160,128]{2,1,0:T(8,128)(2,1)S(1)} %get-tuple-element.79), channel_id=1, source_target_pairs={{0,4},{4,0},{8,12},{12,8},{16,20},{20,16},{24,28},{28,24},{1,5},{5... | collective-permute-start | bytes 491528 | tf_op jit(solution)/shard_map/ppermute | solution.py:35
  67.5 2.1 %collective-permute-start.22 = (bf16[4,160,128]{2,1,0:T(8,128)(2,1)S(1)}, bf16[4,160,128]{2,1,0:T(8,128)(2,1)S(1)}, u32[]{:S(2)}, u32[]{:S(2)}) collective-permute-start(bf16[4,160,128]{2,1,0:T(8,128)(2,1)S(1)} %get-tuple-element.75), channel_id=1, source_target_pairs={{0,4},{4,0},{8,12},{12,8},{16,20},{20,16},{24,28},{28,24},{1,5},{5... | collective-permute-start | bytes 491528 | tf_op jit(solution)/shard_map/ppermute | solution.py:35
  68.9 5.4 %collective-permute-start.30 = (bf16[2,160,128]{2,1,0:T(8,128)(2,1)S(1)}, bf16[2,160,128]{2,1,0:T(8,128)(2,1)S(1)}, u32[]{:S(2)}, u32[]{:S(2)}) collective-permute-start(bf16[2,160,128]{2,1,0:T(8,128)(2,1)S(1)} %get-tuple-element.81), channel_id=1, source_target_pairs={{0,8},{4,12},{8,0},{12,4},{16,24},{20,28},{24,16},{28,20},{1,9},{5... | collective-permute-start | bytes 245768 | tf_op jit(solution)/shard_map/ppermute | solution.py:35
  69.6 7.3 %collective-permute-start.23 = (bf16[2,160,128]{2,1,0:T(8,128)(2,1)S(1)}, bf16[2,160,128]{2,1,0:T(8,128)(2,1)S(1)}, u32[]{:S(2)}, u32[]{:S(2)}) collective-permute-start(bf16[2,160,128]{2,1,0:T(8,128)(2,1)S(1)} %get-tuple-element.77), channel_id=1, source_target_pairs={{0,8},{4,12},{8,0},{12,4},{16,24},{20,28},{24,16},{28,20},{1,9},{5... | collective-permute-start | bytes 245768 | tf_op jit(solution)/shard_map/ppermute | solution.py:35
  74.3 45.7 %copy-start.1 = (bf16[512,2048]{1,0:T(8,128)(2,1)S(1)}, bf16[512,2048]{1,0:T(8,128)(2,1)}, u32[]{:S(2)}) copy-start(bf16[512,2048]{1,0:T(8,128)(2,1)} %refs_6_.1) | copy-start | bytes 6291460
  74.3 45.7 %copy-start.3 = (bf16[512,512]{1,0:T(8,128)(2,1)S(1)}, bf16[512,512]{1,0:T(8,128)(2,1)}, u32[]{:S(2)}) copy-start(bf16[512,512]{1,0:T(8,128)(2,1)} %refs_7_.1) | copy-start | bytes 1572868
  74.3 45.7 %copy-start.5 = (bf16[256,512]{1,0:T(8,128)(2,1)S(1)}, bf16[256,512]{1,0:T(8,128)(2,1)}, u32[]{:S(2)}) copy-start(bf16[256,512]{1,0:T(8,128)(2,1)} %refs_5_.1) | copy-start | bytes 786436
  74.3 8.5 %collective-permute-start.31 = (bf16[2,160,128]{2,1,0:T(8,128)(2,1)S(1)}, bf16[2,160,128]{2,1,0:T(8,128)(2,1)S(1)}, u32[]{:S(2)}, u32[]{:S(2)}) collective-permute-start(bf16[2,160,128]{2,1,0:T(8,128)(2,1)S(1)} %shard_map.112.keep_ref), channel_id=1, source_target_pairs={{0,16},{4,20},{8,24},{12,28},{16,0},{20,4},{24,8},{28,12},{1,17},{... | collective-permute-start | bytes 245768 | tf_op jit(solution)/shard_map/ppermute | solution.py:35
  76.9 6.8 %collective-permute-start.24 = (bf16[2,160,128]{2,1,0:T(8,128)(2,1)S(1)}, bf16[2,160,128]{2,1,0:T(8,128)(2,1)S(1)}, u32[]{:S(2)}, u32[]{:S(2)}) collective-permute-start(bf16[2,160,128]{2,1,0:T(8,128)(2,1)S(1)} %shard_map.109.keep_ref), channel_id=1, source_target_pairs={{0,16},{4,20},{8,24},{12,28},{16,0},{20,4},{24,8},{28,12},{1,17},{... | collective-permute-start | bytes 245768 | tf_op jit(solution)/shard_map/ppermute | solution.py:35
  82.8 4.5 %collective-permute-start.32 = (bf16[2,160,128]{2,1,0:T(8,128)(2,1)S(1)}, bf16[2,160,128]{2,1,0:T(8,128)(2,1)S(1)}, u32[]{:S(2)}, u32[]{:S(2)}) collective-permute-start(bf16[2,160,128]{2,1,0:T(8,128)(2,1)S(1)} %shard_map.113), channel_id=1, source_target_pairs={{0,8},{4,12},{8,0},{12,4},{16,24},{20,28},{24,16},{28,20},{1,9},{5... | collective-permute-start | bytes 245768 | tf_op jit(solution)/shard_map/ppermute | solution.py:35
  83.7 4.5 %collective-permute-start.25 = (bf16[2,160,128]{2,1,0:T(8,128)(2,1)S(1)}, bf16[2,160,128]{2,1,0:T(8,128)(2,1)S(1)}, u32[]{:S(2)}, u32[]{:S(2)}) collective-permute-start(bf16[2,160,128]{2,1,0:T(8,128)(2,1)S(1)} %shard_map.110), channel_id=1, source_target_pairs={{0,8},{4,12},{8,0},{12,4},{16,24},{20,28},{24,16},{28,20},{1,9},{5... | collective-permute-start | bytes 245768 | tf_op jit(solution)/shard_map/ppermute | solution.py:35
  87.4 6.5 %collective-permute-start.33 = (bf16[4,160,128]{2,1,0:T(8,128)(2,1)S(1)}, bf16[4,160,128]{2,1,0:T(8,128)(2,1)S(1)}, u32[]{:S(2)}, u32[]{:S(2)}) collective-permute-start(bf16[4,160,128]{2,1,0:T(8,128)(2,1)S(1)} %pad_maximum_fusion.4.refs_4_), channel_id=1, source_target_pairs={{0,2},{1,3},{2,0},{3,1},{4,6},{5,7},{6,4},{7,5},{8,10},{9,11},{10,... | collective-permute-start | bytes 491528 | tf_op jit(solution)/shard_map/ppermute | solution.py:35
  88.3 7.1 %collective-permute-start.26 = (bf16[4,160,128]{2,1,0:T(8,128)(2,1)S(1)}, bf16[4,160,128]{2,1,0:T(8,128)(2,1)S(1)}, u32[]{:S(2)}, u32[]{:S(2)}) collective-permute-start(bf16[4,160,128]{2,1,0:T(8,128)(2,1)S(1)} %pad_maximum_fusion.3.refs_0_), channel_id=1, source_target_pairs={{0,1},{1,0},{2,3},{3,2},{4,5},{5,4},{6,7},{7,6},{8,9},{9,8},{10,11... | collective-permute-start | bytes 491528 | tf_op jit(solution)/shard_map/ppermute | solution.py:35
  88.9 10.0 %collective-permute-start.34 = (bf16[4,160,128]{2,1,0:T(8,128)(2,1)S(1)}, bf16[4,160,128]{2,1,0:T(8,128)(2,1)S(1)}, u32[]{:S(2)}, u32[]{:S(2)}) collective-permute-start(bf16[4,160,128]{2,1,0:T(8,128)(2,1)S(1)} %pad_maximum_fusion.4.refs_4_), channel_id=1, source_target_pairs={{0,1},{1,0},{2,3},{3,2},{4,5},{5,4},{6,7},{7,6},{8,9},{9,8},{10,11... | collective-permute-start | bytes 491528 | tf_op jit(solution)/shard_map/ppermute | solution.py:35
  90.3 8.6 %collective-permute-start.27 = (bf16[4,160,128]{2,1,0:T(8,128)(2,1)S(1)}, bf16[4,160,128]{2,1,0:T(8,128)(2,1)S(1)}, u32[]{:S(2)}, u32[]{:S(2)}) collective-permute-start(bf16[4,160,128]{2,1,0:T(8,128)(2,1)S(1)} %pad_maximum_fusion.3.refs_0_), channel_id=1, source_target_pairs={{0,2},{1,3},{2,0},{3,1},{4,6},{5,7},{6,4},{7,5},{8,10},{9,11},{10,... | collective-permute-start | bytes 491528 | tf_op jit(solution)/shard_map/ppermute | solution.py:35
  91.6 16.3 %collective-permute-start.19 = (bf16[256,640]{1,0:T(8,128)(2,1)S(1)}, bf16[256,640]{1,0:T(8,128)(2,1)S(1)}, u32[]{:S(2)}, u32[]{:S(2)}) collective-permute-start(bf16[256,640]{1,0:T(8,128)(2,1)S(1)} %get-tuple-element.68), channel_id=1, source_target_pairs={{0,1},{1,0},{2,3},{3,2},{4,5},{5,4},{6,7},{7,6},{8,9},{9,8},{10,11... | collective-permute-start | bytes 983048 | tf_op jit(solution)/shard_map/ppermute | solution.py:35
  99.0 23.4 %collective-permute-start.37 = (bf16[16,160,128]{2,1,0:T(8,128)(2,1)S(1)}, bf16[16,160,128]{2,1,0:T(8,128)(2,1)S(1)}, u32[]{:S(2)}, u32[]{:S(2)}) collective-permute-start(bf16[16,160,128]{2,1,0:T(8,128)(2,1)S(1)} %pad_maximum_fusion), channel_id=1, source_target_pairs={{0,4},{4,0},{8,12},{12,8},{16,20},{20,16},{24,28},{28,24},{1,5},{5... | collective-permute-start | bytes 1966088 | tf_op jit(solution)/shard_map/ppermute | solution.py:35
  99.1 7.4 %collective-permute-start.35 = (bf16[4,160,128]{2,1,0:T(8,128)(2,1)S(1)}, bf16[4,160,128]{2,1,0:T(8,128)(2,1)S(1)}, u32[]{:S(2)}, u32[]{:S(2)}) collective-permute-start(bf16[4,160,128]{2,1,0:T(8,128)(2,1)S(1)} %collective-permute-done.33.refs_5_), channel_id=1, source_target_pairs={{0,1},{1,0},{2,3},{3,2},{4,5},{5,4},{6,7},{7,6},{8,9},{9,8},{10,11... | collective-permute-start | bytes 491528 | tf_op jit(solution)/shard_map/ppermute | solution.py:35
  99.7 8.2 %collective-permute-start.28 = (bf16[4,160,128]{2,1,0:T(8,128)(2,1)S(1)}, bf16[4,160,128]{2,1,0:T(8,128)(2,1)S(1)}, u32[]{:S(2)}, u32[]{:S(2)}) collective-permute-start(bf16[4,160,128]{2,1,0:T(8,128)(2,1)S(1)} %collective-permute-done.26.refs_1_), channel_id=1, source_target_pairs={{0,2},{1,3},{2,0},{3,1},{4,6},{5,7},{6,4},{7,5},{8,10},{9,11},{10,... | collective-permute-start | bytes 491528 | tf_op jit(solution)/shard_map/ppermute | solution.py:35
  100.9 19.1 %collective-permute-start.20 = (bf16[256,640]{1,0:T(8,128)(2,1)S(1)}, bf16[256,640]{1,0:T(8,128)(2,1)S(1)}, u32[]{:S(2)}, u32[]{:S(2)}) collective-permute-start(bf16[256,640]{1,0:T(8,128)(2,1)S(1)} %get-tuple-element.69), channel_id=1, source_target_pairs={{0,2},{1,3},{2,0},{3,1},{4,6},{5,7},{6,4},{7,5},{8,10},{9,11},{10,... | collective-permute-start | bytes 983048 | tf_op jit(solution)/shard_map/ppermute | solution.py:35
  106.5 13.5 %collective-permute-start.21 = (bf16[256,640]{1,0:T(8,128)(2,1)S(1)}, bf16[256,640]{1,0:T(8,128)(2,1)S(1)}, u32[]{:S(2)}, u32[]{:S(2)}) collective-permute-start(bf16[256,640]{1,0:T(8,128)(2,1)S(1)} %get-tuple-element.70), channel_id=1, source_target_pairs={{0,3},{1,2},{2,1},{3,0},{4,7},{5,6},{6,5},{7,4},{8,11},{9,10},{10,... | collective-permute-start | bytes 983048 | tf_op jit(solution)/shard_map/ppermute | solution.py:35
  107.9 14.6 %collective-permute-start.36 = (bf16[8,160,128]{2,1,0:T(8,128)(2,1)S(1)}, bf16[8,160,128]{2,1,0:T(8,128)(2,1)S(1)}, u32[]{:S(2)}, u32[]{:S(2)}) collective-permute-start(bf16[8,160,128]{2,1,0:T(8,128)(2,1)S(1)} %pad_maximum_fusion.1), channel_id=1, source_target_pairs={{0,4},{4,0},{8,12},{12,8},{16,20},{20,16},{24,28},{28,24},{1,5},{5... | collective-permute-start | bytes 983048 | tf_op jit(solution)/shard_map/ppermute | solution.py:35
  107.9 14.5 %collective-permute-start.38 = (bf16[8,160,128]{2,1,0:T(8,128)(2,1)S(1)}, bf16[8,160,128]{2,1,0:T(8,128)(2,1)S(1)}, u32[]{:S(2)}, u32[]{:S(2)}) collective-permute-start(bf16[8,160,128]{2,1,0:T(8,128)(2,1)S(1)} %pad_maximum_fusion.2), channel_id=1, source_target_pairs={{0,4},{4,0},{8,12},{12,8},{16,20},{20,16},{24,28},{28,24},{1,5},{5... | collective-permute-start | bytes 983048 | tf_op jit(solution)/shard_map/ppermute | solution.py:35
